TPU v7x, 32 devices: a whole 2x2x4 slice. The times are simulated.
32 devices in a mesh: ctx: 16 (over z, x, core), fsdp: 2 (over y).
Axes of the slice: x: 2, y: 2, z: 4, core: 2. Of those that a mesh axis runs over, the one named last changes fastest.
Arguments:
- hidden_in: bfloat16 [2, 2048, 1024], P('fsdp', 'ctx'), may hold values from -6 to 6
- out_grad: bfloat16 [2, 2048, 1024], P('fsdp', 'ctx'), may hold values from -6 to 6
- doc_lengths: int32 [2, 16], P('fsdp'), may hold values from 1 to 512, 2048 in all within a row
- block_order: int32 [2, 32], P('fsdp'), may hold values from 0 to 31, as said below
- routes: int32 [2, 2048, 8], P('fsdp', 'ctx'), may hold values from 0 to 15, all different within a row
- attn_norm: bfloat16 [1024], P(('ctx', 'fsdp')), may hold values from 0.5 to 1.5
- w_query: bfloat16 [1024, 1024], P(('ctx', 'fsdp')), may hold values from -0.625 to 0.625
- w_key: bfloat16 [1024, 512], P(('ctx', 'fsdp')), may hold values from -0.625 to 0.625
- w_value: bfloat16 [1024, 512], P(('ctx', 'fsdp')), may hold values from -0.1875 to 0.1875
- w_output: bfloat16 [1024, 1024], P(('ctx', 'fsdp')), may hold values from -3 to 3
- ffn_norm: bfloat16 [1024], P(('ctx', 'fsdp')), may hold values from 0.5 to 1.5
- w_router: bfloat16 [1024, 16], P(('ctx', 'fsdp')), may hold values from -0.09375 to 0.09375
- w_gate_up: bfloat16 [1024, 16384], P(('ctx', 'fsdp')), may hold values from -0.1875 to 0.1875
- w_down: bfloat16 [1024, 8192], P(('ctx', 'fsdp')), may hold values from -4 to 4
Outputs:
- hidden_out: bfloat16 [2, 2048, 1024], P('fsdp', 'ctx')
- grad_in: float32 [2, 2048, 1024], P('fsdp', 'ctx')
- grad_attn_norm: float32 [1024], P(('ctx', 'fsdp'))
- grad_query: float32 [1024, 1024], P(('ctx', 'fsdp'))
- grad_key: float32 [1024, 512], P(('ctx', 'fsdp'))
- grad_value: float32 [1024, 512], P(('ctx', 'fsdp'))
- grad_output: float32 [1024, 1024], P(('ctx', 'fsdp'))
- grad_ffn_norm: float32 [1024], P(('ctx', 'fsdp'))
- grad_router: float32 [1024, 16], P(('ctx', 'fsdp'))
- grad_gate_up: float32 [1024, 16384], P(('ctx', 'fsdp'))
- grad_down: float32 [1024, 8192], P(('ctx', 'fsdp'))
Inputs may be any that keep to these rules, and one draw needn't show every extreme that they name: `block_order`: in each sequence, storage blocks 2 c and 2 c + 1 (those of ctx index c) hold the sequence blocks p and 31 - p, in either order; every sequence block is held once. `doc_lengths`: each row sums to 2048; the longest document has exactly 512 tokens. `routes`: each token names 8 different experts; every expert is named by some token.
All inputs are finite; a program needn't handle non-finite values.
Results may differ from a plain program's by a relative error of at most 0.017.
Values may be sent and summed in bfloat16 or wider, within the bound.
No kernel may reach another device: no remote copies, remote signals or barrier semaphores. Data moves between devices by JAX's collectives and lax.ppermute only.
A program may use at most 320 MiB of HBM per device.

v0:
```python
import functools

import jax
import jax.numpy as jnp
import numpy as np
from jax import lax
from jax.experimental import pallas as pl
from jax.experimental.pallas import tpu as pltpu
from jax.sharding import PartitionSpec as P

D = 1024
H = 16
KVH = 8
HD = 64
F = 512
E = 16

EPSILON = 1e-06
SCORE_SCALE = 0.015625
RESIDUAL_SCALE = 0.22
THETA = 10000.0
NEGATIVE = -1e30
BOTH = ("ctx", "fsdp")
EXPERT_WEIGHT = 2
BF = jnp.bfloat16
F32 = jnp.float32
QUERY_BLOCK = 256


def dot(left, right, left_dim, right_dim):
    return lax.dot_general(
        left, right, (((left_dim,), (right_dim,)), ((), ())), preferred_element_type=F32
    )


def permute(values, pairs):
    return lax.ppermute(values, "ctx", pairs)


def shift_z(step):
    return [(i, ((i // 4 + step) % 4) * 4 + i % 4) for i in range(16)]


SWAP_X = [(i, i ^ 2) for i in range(16)]
SWAP_CORE = [(i, i ^ 1) for i in range(16)]


def after(value, *others):
    return lax.optimization_barrier((value, *others))[0] if others else lax.optimization_barrier(value)


def block_order_of(count):
    index = jnp.arange(count, dtype=jnp.int32)
    if lax.axis_size("ctx") != 16:
        return index
    place = lax.axis_index("ctx")
    z_of = (place // 4 - (index % 8) // 2 + 4) % 4
    x_of = ((place // 2) % 2 + index % 2) % 2
    return z_of * 4 + x_of * 2 + (place % 2 + index // 8) % 2


class RingSum:
    def __init__(self, mine, arrived):
        self.mine, self.arrived = mine, arrived
        self.count = mine.shape[0] // 8
        self.cross_out = jnp.concatenate([self.chip(k, 1) for k in (2, 1, 3)], 0).astype(BF)

    def chip(self, k, dx):
        rows = slice((2 * k + dx) * self.count, (2 * k + dx + 1) * self.count)
        return self.mine[rows].astype(F32) + self.arrived[rows].astype(F32)

    def cross(self):
        got = permute(self.cross_out, SWAP_X)
        self.sends = []
        for j, k in enumerate((2, 1, 3)):
            term = got[j * self.count : (j + 1) * self.count].astype(F32)
            self.sends.append((self.chip(k, 0) + term).astype(BF))

    def end(self, *others):
        self.own = permute(self.chip(0, 1).astype(BF), SWAP_X)
        total = self.chip(0, 0) + self.own.astype(F32)
        for send, k in zip(self.sends, (2, 1, 3)):
            term = permute(send, shift_z(4 - k))
            self.seen = term
            if k == 2 and others:
                term = after(term, *others)
            total = total + term.astype(F32)
        return total


def join_kernel(places, *refs):
    pieces, out_ref, sems = refs[:14], refs[14], refs[15]
    count = out_ref.shape[1]
    copies = []
    for side in range(2):
        own, far, one, pair, two, far_two, three = pieces[7 * side : 7 * side + 7]
        lower, upper = pair.at[:count], pair.at[count:]
        for j, piece in enumerate((own, far, one, lower, two, far_two, three, upper)):
            block = 8 * side + j
            copies.append(
                pltpu.make_async_copy(piece, out_ref.at[places[block]], sems.at[block])
            )
    for copy in copies:
        copy.start()
    for copy in copies:
        copy.wait()


def spread_ctx(blocks):
    _, rows, width = blocks.shape
    other = permute(blocks[8:], SWAP_CORE)
    chip = jnp.stack([blocks[:8], other], 1).reshape(4, 2, 2, rows, width)
    crossed = permute(chip[:, 1], SWAP_X)
    both = jnp.concatenate([chip[:, 0], crossed], 1)
    return (both[0], *(permute(both[k], shift_z(4 - k)) for k in range(1, 4)))


def sender_order_of():
    place = lax.axis_index("ctx")
    index = jnp.arange(16, dtype=jnp.int32)
    z_of = (place // 4 + index // 4) % 4
    x_of = ((place // 2) % 2 + (index // 2) % 2) % 2
    return z_of * 4 + x_of * 2 + (place % 2 + index % 2) % 2


class Gather:
    def __init__(self, rows):
        self.count = rows.shape[0]
        self.own = rows
        self.one = permute(rows, shift_z(1))
        self.three = permute(rows, shift_z(3))
        self.far = permute(rows, SWAP_X)
        self.two = permute(rows, shift_z(2))

    def cross(self, *others):
        if others:
            self.one, self.three = after((self.one, self.three), *others)
        self.pair = permute(jnp.concatenate([self.one, self.three], 0), SWAP_X)

    def last(self, *others):
        if others:
            self.two = after(self.two, *others)
        self.far_two = permute(self.two, SWAP_X)

    def join(self, places, name, *others):
        if others:
            self.far, self.far_two = after((self.far, self.far_two), *others)
        mine = (self.own, self.far, self.one, self.pair, self.two, self.far_two, self.three)
        other = tuple(permute(piece, SWAP_CORE) for piece in mine)
        shape = (16, *self.own.shape)
        return pl.pallas_call(
            join_kernel,
            out_shape=jax.ShapeDtypeStruct(shape, BF),
            grid_spec=pltpu.PrefetchScalarGridSpec(
                num_scalar_prefetch=1,
                grid=(1,),
                in_specs=[fixed(piece.shape) for piece in (*mine, *other)],
                out_specs=pl.BlockSpec(memory_space=pl.ANY),
                scratch_shapes=[pltpu.SemaphoreType.DMA((16,))],
            ),
            compiler_params=params(),
            cost_estimate=cost(1, 4 * self.own.size * 16),
            name=name,
        )(places, *mine, *other)


def tables_of(total):
    half_width = HD // 2
    frequency = (THETA ** (-np.arange(half_width) / half_width)).astype(np.float32)
    angles = np.arange(total, dtype=np.float32)[:, None] * frequency[None, :]
    cosine = np.cos(angles.astype(np.float64)).astype(np.float32)
    sine = np.sin(angles.astype(np.float64)).astype(np.float32)
    return jnp.asarray(np.tile(cosine, (1, 4))), jnp.asarray(np.tile(sine, (1, 4)))


def window_of(step, band):
    start = jnp.maximum(step * QUERY_BLOCK - band, 0)
    return pl.multiple_of(start, QUERY_BLOCK), pl.multiple_of(step * QUERY_BLOCK, QUERY_BLOCK)


def masked_scores(queries, keys_win, first_key, first_query, firsts):
    raw = dot(queries, keys_win, 1, 1) * SCORE_SCALE
    key_place = first_key + lax.broadcasted_iota(jnp.int32, raw.shape, 1)
    query_place = first_query + lax.broadcasted_iota(jnp.int32, raw.shape, 0)
    column = first_query + lax.broadcasted_iota(jnp.int32, (raw.shape[0], 1), 0)
    start = jnp.zeros_like(column)
    for j in range(1, firsts.shape[0]):
        start = jnp.where(firsts[j] <= column, jnp.maximum(start, firsts[j]), start)
    visible = (key_place <= query_place) & (key_place >= start)
    return jnp.where(visible, raw, NEGATIVE)


def lanes_of(values):
    return lax.broadcasted_iota(jnp.int32, values.shape, 1)


def fixed(shape, at=None):
    place = (0,) * len(shape) if at is None else at
    return pl.BlockSpec(shape, lambda *_: place, pipeline_mode=pl.Buffered(1))


def params(mib=56):
    return pltpu.CompilerParams(vmem_limit_bytes=mib * 2**20)


def cost(flops, bytes_accessed, transcendentals=0, weight=20):
    return pl.CostEstimate(
        flops=weight * flops,
        bytes_accessed=weight * bytes_accessed,
        transcendentals=transcendentals,
    )


def column_of(row_ref):
    return jnp.broadcast_to(row_ref[:1, :], (128, row_ref.shape[1])).T


def pack_kernel(copies, wq_ref, wk_ref, wv_ref, wr_ref, norm_ref, small_ref):
    rows = wq_ref.shape[0]
    rest = jnp.concatenate(
        [wr_ref[...], norm_ref[...], jnp.zeros((rows, HD - E - 2), BF)], axis=1
    )
    for place in range(E * copies):
        head = place // copies
        pair = head // (H // KVH)
        query = wq_ref[:, head * HD : (head + 1) * HD]
        key = wk_ref[:, pair * HD : (pair + 1) * HD]
        value = wv_ref[:, pair * HD : (pair + 1) * HD]
        small_ref[place] = jnp.concatenate([query, key, value, rest], axis=1)


def pack_small(copies, *weights):
    shape = (E * copies, weights[0].shape[0], 256)
    return pl.pallas_call(
        functools.partial(pack_kernel, copies),
        out_shape=jax.ShapeDtypeStruct(shape, BF),
        grid=(1,),
        in_specs=[fixed(weight.shape) for weight in weights],
        out_specs=fixed(shape),
        compiler_params=params(),
        cost_estimate=cost(1, 2**20),
        name="pack_small",
    )(*weights)


def split_kernel(small_ref, ext_ref, head_ref, router_ref, one_ref, two_ref):
    small = small_ref[...]
    wq, wk, wv = (small[:, j * HD : (j + 1) * HD] for j in range(3))
    turn = HD // 2
    zero = jnp.zeros_like(wv)
    rest = small[:, 3 * HD :]
    ext_ref[:, :128] = small[:, :128]
    ext_ref[:, 128:256] = jnp.concatenate(
        [-wq[:, turn:], wq[:, :turn], -wk[:, turn:], wk[:, :turn]], 1
    )
    value = jnp.concatenate([wv, zero], 1)
    ext_ref[:, 256:] = value
    head_ref[:, :128] = small[:, :128]
    head_ref[:, 128:] = value
    rest = jnp.concatenate([rest, zero], 1).astype(F32)
    router_ref[...] = jnp.where(lanes_of(rest) < E, rest, 0.0).astype(BF)
    turned = rest.T
    one_ref[...] = turned[E : E + 1, :]
    two_ref[...] = turned[E + 1 : E + 2, :]


def split_small(small):
    shapes = ((D, 384), (D, 256), (D, 128), (1, D), (1, D))
    types = (BF, BF, BF, F32, F32)
    return pl.pallas_call(
        split_kernel,
        out_shape=tuple(jax.ShapeDtypeStruct(s, t) for s, t in zip(shapes, types)),
        grid=(1,),
        in_specs=[fixed(small.shape)],
        out_specs=tuple(fixed(s) for s in shapes),
        compiler_params=params(),
        cost_estimate=cost(1, 3 * 2**20),
        name="split_weights",
    )(small)


def project(x_blk, w_ref, gain_ref, cosine, sine):
    x_f = x_blk.astype(F32)
    factor = lax.rsqrt(jnp.mean(x_f * x_f, axis=1, keepdims=True) + EPSILON)
    normed = (x_f * factor * gain_ref[...]).astype(BF)
    out = dot(normed, w_ref[...], 1, 0)
    both = out[:, :128] * cosine + out[:, 128:256] * sine
    swapped = pltpu.roll(both, 64, 1)
    low = lanes_of(both) < HD
    zero = jnp.zeros_like(both)
    return jnp.concatenate(
        [
            jnp.where(low, both, zero).astype(BF),
            jnp.where(low, swapped, zero).astype(BF),
            jnp.where(low, zero, swapped).astype(BF),
            out[:, 256:].astype(BF),
        ],
        axis=1,
    )


def spot_of(ids, block, block_len):
    return pl.ds(pl.multiple_of(ids[block] * block_len, block_len), block_len)


def head_kernel(
    block_len, band, ids, spots, firsts,
    x_ref, w_ref, gain_ref, cos_ref, sin_ref, all_ref, log_ref, att_ref, a_store,
):
    step = pl.program_id(0)
    total = all_ref.shape[0]
    blocks = QUERY_BLOCK // block_len

    places = [spot_of(ids, 4 * step + j, block_len) for j in range(4)]
    cosine = jnp.concatenate([cos_ref[spot, :] for spot in places], 0)
    sine = jnp.concatenate([sin_ref[spot, :] for spot in places], 0)
    made = project(x_ref[...], w_ref, gain_ref, cosine, sine)
    for j in range(4):
        all_ref[places[j], :] = made[j * block_len : (j + 1) * block_len]

    @pl.when(step == pl.num_programs(0) - 1)
    def _():
        window = band + QUERY_BLOCK

        def step_fn(index, carry):
            first_key, first_query = window_of(index, band)
            rows = pl.ds(first_query, QUERY_BLOCK)
            cols = pl.ds(first_key, window)
            scores = masked_scores(
                all_ref[rows, :128], all_ref[cols, 128:256], first_key, first_query, firsts
            )
            top = jnp.max(scores, axis=1, keepdims=True)
            weight = jnp.exp(scores - top)
            mass = jnp.sum(weight, axis=1, keepdims=True)
            log_ref[rows, :] = top + jnp.log(mass)
            weight = (weight * (1.0 / mass)).astype(BF)
            result = dot(weight, all_ref[cols, 384:], 1, 0)
            for j in range(blocks):
                spot = spot_of(spots, index * blocks + j, block_len)
                a_store[spot, :] = result[j * block_len : (j + 1) * block_len]
            return carry

        lax.fori_loop(0, total // QUERY_BLOCK, step_fn, 0)
        for j in range(total // QUERY_BLOCK):
            part = a_store[j * QUERY_BLOCK : (j + 1) * QUERY_BLOCK, :]
            att_ref[:, j * QUERY_BLOCK : (j + 1) * QUERY_BLOCK] = part.T[:HD].astype(BF)


def head_forward(hidden, w_ext, gain, tables, ids, spots, firsts, count, band):
    total = tables[0].shape[0]
    work = total * (band + QUERY_BLOCK)
    return pl.pallas_call(
        functools.partial(head_kernel, count // 2, band),
        out_shape=(
            jax.ShapeDtypeStruct((total, 512), BF),
            jax.ShapeDtypeStruct((total, 1), F32),
            jax.ShapeDtypeStruct((HD, total), BF),
        ),
        grid_spec=pltpu.PrefetchScalarGridSpec(
            num_scalar_prefetch=3,
            grid=(total // count // 2,),
            in_specs=[
                pl.BlockSpec((2 * count, D), lambda i, *_: (i, 0)),
                fixed((D, 384)), fixed((1, D)), fixed((total, 128)), fixed((total, 128)),
            ],
            out_specs=(fixed((total, 512)), fixed((total, 1)), fixed((HD, total))),
            scratch_shapes=[pltpu.VMEM((total, 128), F32)],
        ),
        compiler_params=params(),
        cost_estimate=cost(total * D * 384 + 4 * work * 128, 2 * total * D, work),
        name="head_forward",
    )(ids, spots, firsts, hidden, w_ext, gain, *tables)


def order_heads(heads, wo_ref, wo_rel):
    per = wo_ref.shape[1]
    many = HD // per
    for j in range(H):
        for m in range(many):
            wo_rel[j * HD + m * per : j * HD + (m + 1) * per, :] = wo_ref[heads[j] * many + m]


def back_kernel(
    part, tok_count, heads, where, att_ref, x_ref, g_ref, wo_ref, wgu_ref, wd_ref, wr_ref,
    gain_ref, act_ref, v_ref, pa_ref, pb_ref, grads_ref, mid_ref, wo_rel, gb_ref, norm_ref, acc, scr,
):
    step = pl.program_id(0)
    own_expert = where[0]
    half = D // 2

    @pl.when(step == 0)
    def _():
        order_heads(heads, wo_ref, wo_rel)
        norm_ref[...] = jnp.zeros_like(norm_ref)

    tile = x_ref.shape[0]
    moved = dot(att_ref[...].reshape(D, tile), wo_ref[...].reshape(D, D), 0, 0)
    middle = x_ref[...].astype(F32) + RESIDUAL_SCALE * moved
    scr[...] = middle

    @pl.when(step == where[2] * tok_count // tile)
    def _():
        own = pl.multiple_of(where[2] * tok_count % tile, tok_count)
        mid_ref[...] = scr[pl.ds(own, tok_count), :]

    gain = gain_ref[...]
    factor = lax.rsqrt(jnp.mean(middle * middle, axis=1, keepdims=True) + EPSILON)
    mixed = (middle * factor * gain).astype(BF)
    grads = g_ref[...].reshape(mixed.shape[0], D + 128)
    logits = dot(mixed, wr_ref[...], 1, 0)
    mask = grads[:, D:].astype(F32)
    logits = jnp.where(mask > 0.0, logits, NEGATIVE)
    odds = jnp.where(mask > 0.0, jnp.exp(logits - jnp.max(logits, axis=1, keepdims=True)), 0.0)
    combine = odds / jnp.sum(odds, axis=1, keepdims=True)
    mark = (lanes_of(combine) == own_expert).astype(F32)
    own_gate = jnp.sum(combine * mark, axis=1, keepdims=True)
    grad_top = grads[:, :D]
    pulled = RESIDUAL_SCALE * dot(grad_top, wd_ref[...], 1, 0)
    gates = dot(mixed, wgu_ref[...], 1, 0)
    gate, up = gates[:, :part], gates[:, part:]
    sigma = 1.0 / (1.0 + jnp.exp(-gate))
    silu = gate * sigma
    activation = silu * up
    grad_act = own_gate * pulled
    act = (RESIDUAL_SCALE * own_gate * activation).astype(BF)
    act_ref[...] = act
    gb_ref[:, :part] = (grad_act * up * sigma * (1.0 + gate * (1.0 - sigma))).astype(BF)
    gb_ref[:, part:] = (grad_act * silu).astype(BF)
    grad_combine = jnp.sum(activation * pulled, axis=1, keepdims=True)
    coef = (grad_combine * own_gate * (mark - combine)).astype(BF)
    terms = (
        (0, 2 * part, mixed, gb_ref[...]),
        (2 * part, 2 * part + 128, mixed, coef),
        (2 * part + 128, 3 * part + 128, grad_top, act),
    )

    @pl.when(step == 0)
    def _():
        for low, high, left, right in terms:
            acc[:, low:high] = dot(left, right, 0, 0)

    @pl.when(step > 0)
    def _():
        for low, high, left, right in terms:
            acc[:, low:high] += dot(left, right, 0, 0)

    grad_mixed = dot(gb_ref[...], wgu_ref[...], 1, 1) + dot(coef, wr_ref[...], 1, 1)
    scaled = scr[...] * factor
    norm_ref[...] += jnp.broadcast_to(
        jnp.sum(grad_mixed * scaled, axis=0, keepdims=True), norm_ref.shape
    )
    inner = grad_mixed * gain
    grad_mid = factor * (inner - scaled * jnp.mean(inner * scaled, axis=1, keepdims=True))
    grad_mid = grad_mid.astype(BF)
    v_ref[...] = grad_mid
    out_grads = dot(wo_rel[...], grad_mid, 1, 1)
    if part == F:
        top = out_grads[:HD] + dot(wo_rel[:HD, :], grad_top, 1, 1)
        pa_ref[:HD, :] = (RESIDUAL_SCALE * top).astype(BF)
        pa_ref[HD:, :] = (RESIDUAL_SCALE * out_grads[HD:half]).astype(BF)
    else:
        pa_ref[...] = (RESIDUAL_SCALE * out_grads[:half]).astype(BF)
    pb_ref[...] = (RESIDUAL_SCALE * out_grads[half:]).astype(BF)

    @pl.when(step == pl.num_programs(0) - 1)
    def _():
        middle = slice(2 * part, 2 * part + 128)
        last = acc[:, middle]
        grads_ref[:, : 2 * part] = acc[:, : 2 * part].astype(BF)
        grads_ref[:, middle] = jnp.where(lanes_of(last) == E, column_of(norm_ref), last).astype(BF)
        grads_ref[:, 2 * part + 128 :] = acc[:, 2 * part + 128 :].astype(BF)


def expert_main(att, hidden, top, wo, wgu, wd, wr, gain, heads, where, count):
    total = hidden.shape[0]
    part = wd.shape[1]
    tile = 2 * count
    width = 3 * part + 128

    def rows(size):
        return pl.BlockSpec((tile, size), lambda i, *_: (i, 0))

    def cols(height):
        return pl.BlockSpec((height, tile), lambda i, *_: (0, i))

    def out(size):
        return jax.ShapeDtypeStruct((total, size), BF)

    half = jax.ShapeDtypeStruct((D // 2, total), BF)
    return pl.pallas_call(
        functools.partial(back_kernel, part, count),
        out_shape=(
            out(part), out(D), half, half, jax.ShapeDtypeStruct((D, width), BF),
            jax.ShapeDtypeStruct((count, D), F32),
        ),
        grid_spec=pltpu.PrefetchScalarGridSpec(
            num_scalar_prefetch=2,
            grid=(total // tile,),
            in_specs=[
                pl.BlockSpec((H, HD, tile), lambda i, *_: (0, 0, i)),
                rows(D),
                pl.BlockSpec((2, count, D + 128), lambda i, *_: (i, 0, 0)),
                fixed(wo.shape), fixed((D, 2 * part)), fixed((D, part)), fixed((D, 128)),
                fixed((1, D)),
            ],
            out_specs=(
                rows(part), rows(D), cols(D // 2), cols(D // 2), fixed((D, width)),
                fixed((count, D)),
            ),
            scratch_shapes=[
                pltpu.VMEM((D, D), BF),
                pltpu.VMEM((tile, 2 * part), BF),
                pltpu.VMEM((8, D), F32),
                pltpu.VMEM((D, width), F32),
                pltpu.VMEM((tile, D), F32),
            ],
        ),
        compiler_params=params(),
        cost_estimate=cost(
            2 * total * D * (2 * D + 8 * part), 12 * total * D, total * part, weight=EXPERT_WEIGHT
        ),
        name="expert_main",
    )(heads, where, att, hidden, top, wo, wgu, wd, wr, gain)


def moe_kernel(act_ref, wd_ref, out_ref):
    out_ref[...] = dot(act_ref[...], wd_ref[...], 1, 1).astype(BF).reshape(out_ref.shape)


def moe_out(act, wd, count, rows):
    total, part = act.shape
    many = 4
    return pl.pallas_call(
        moe_kernel,
        out_shape=jax.ShapeDtypeStruct((total // count, count + 2 * rows, D), BF),
        grid=(total // count // many,),
        in_specs=[pl.BlockSpec((many * count, part), lambda i: (i, 0)), fixed((D, part))],
        out_specs=pl.BlockSpec((many, count, D), lambda i: (i, 0, 0)),
        compiler_params=params(),
        cost_estimate=cost(2 * total * D * part, 3 * total * D),
        name="moe_out",
    )(act, wd)


def output_kernel(where, att_ref, v_ref, g_ref, moe_ref, out_ref, acc):
    step = pl.program_id(0)
    tile = v_ref.shape[0]

    @pl.when(step == 0)
    def _():
        acc[...] = jnp.zeros_like(acc)

    acc[...] += dot(att_ref[...].reshape(D, tile), v_ref[...], 1, 0)
    picked = att_ref[where[0]]
    place = step * tile + lanes_of(picked)
    picked = jnp.where(place // where[3] == where[1], picked, jnp.zeros_like(picked))
    target = pl.ds(pl.multiple_of(where[0] * HD, HD), HD)
    acc[target, :] += dot(picked, g_ref[...].reshape(tile, D), 1, 0)

    @pl.when(step == pl.num_programs(0) - 1)
    def _():
        out_ref[...] = (RESIDUAL_SCALE * acc[...]).astype(BF).reshape(out_ref.shape)


def output_weights(att, grad_mid, top, moe, where, count, rows):
    total = grad_mid.shape[0]
    tile = 4 * count
    per = 2 * rows
    return pl.pallas_call(
        output_kernel,
        out_shape=jax.ShapeDtypeStruct(moe.shape, BF),
        grid_spec=pltpu.PrefetchScalarGridSpec(
            num_scalar_prefetch=1,
            grid=(total // tile,),
            in_specs=[
                pl.BlockSpec((H, HD, tile), lambda i, *_: (0, 0, i)),
                pl.BlockSpec((tile, D), lambda i, *_: (i, 0)),
                pl.BlockSpec((4, count, D), lambda i, *_: (i, 0, 0)),
                pl.BlockSpec(memory_space=pl.ANY),
            ],
            out_specs=fixed((moe.shape[0], per, D), (0, count // per, 0)),
            scratch_shapes=[pltpu.VMEM((D, D), F32)],
        ),
        input_output_aliases={4: 0},
        compiler_params=params(),
        cost_estimate=cost(2 * total * D * D, 8 * total * D),
        name="output_weights",
    )(where, att, grad_mid, top, moe)


def attend_kernel(
    block_len, band, ids, spots, firsts, where, all_ref, up_ref, log_ref, cos_ref, sin_ref,
    own_ref, up_sort, acc_qk, acc_v,
):
    total = all_ref.shape[0]
    blocks = QUERY_BLOCK // block_len
    window = band + QUERY_BLOCK
    acc_qk[...] = jnp.zeros_like(acc_qk)
    acc_v[...] = jnp.zeros_like(acc_v)
    for j in range(total // QUERY_BLOCK):
        piece = up_ref[:, j * QUERY_BLOCK : (j + 1) * QUERY_BLOCK]
        piece = jnp.concatenate([piece, jnp.zeros_like(piece)], 0).T.astype(BF)
        for m in range(blocks):
            spot = spot_of(ids, j * blocks + m, block_len)
            up_sort[spot, :] = piece[m * block_len : (m + 1) * block_len]

    def step_fn(index, carry):
        first_key, first_query = window_of(index, band)
        rows = pl.ds(first_query, QUERY_BLOCK)
        cols = pl.ds(first_key, window)
        keys_win, upstream = all_ref[cols, 128:256], up_sort[rows, :]
        scores = masked_scores(all_ref[rows, :128], keys_win, first_key, first_query, firsts)
        weight = jnp.exp(scores - log_ref[rows, :])
        grad_weight = dot(upstream, all_ref[cols, 384:], 1, 1)
        delta = jnp.sum(weight * grad_weight, axis=1, keepdims=True)
        grad_raw = (SCORE_SCALE * weight * (grad_weight - delta)).astype(BF)
        acc_qk[rows, :] += dot(grad_raw, keys_win, 1, 0)
        acc_qk[cols, :] += dot(grad_raw, all_ref[rows, 256:384], 0, 0)
        acc_v[cols, :] += dot(weight.astype(BF), upstream, 0, 0)
        return carry

    lax.fori_loop(0, total // QUERY_BLOCK, step_fn, 0)

    def turn(index, carry):
        first = pl.multiple_of(index * QUERY_BLOCK, QUERY_BLOCK)
        rows = pl.ds(first, QUERY_BLOCK)
        both = acc_qk[rows, :]
        low = lanes_of(both) % HD < HD // 2
        swapped = jnp.where(low, pltpu.roll(both, 96, 1), -pltpu.roll(both, 32, 1))
        turned = (both * cos_ref[rows, :] + swapped * sin_ref[rows, :]).astype(BF)
        made = jnp.concatenate([turned, acc_v[rows, :].astype(BF)], 1)
        for j in range(blocks):
            block = spots[index * blocks + j]
            first = pl.multiple_of(block * block_len, block_len)
            piece = made[j * block_len : (j + 1) * block_len]
            keep = first // where[3] == where[1]
            own_ref[pl.ds(first, block_len), :] = jnp.where(keep, piece, jnp.zeros_like(piece))
        return carry

    lax.fori_loop(0, total // QUERY_BLOCK, turn, 0)


def attend_backward(heads_all, upstream, logs, tables, ids, spots, firsts, where, count, band):
    total = heads_all.shape[0]
    work = total * (band + QUERY_BLOCK)
    return pl.pallas_call(
        functools.partial(attend_kernel, count // 2, band),
        out_shape=jax.ShapeDtypeStruct((total, 256), BF),
        grid_spec=pltpu.PrefetchScalarGridSpec(
            num_scalar_prefetch=4,
            grid=(1,),
            in_specs=[
                fixed((total, 512)), fixed((HD, total)), fixed((total, 1)), fixed((total, 128)),
                fixed((total, 128)),
            ],
            out_specs=fixed((total, 256)),
            scratch_shapes=[
                pltpu.VMEM((total, 128), BF),
                pltpu.VMEM((total, 128), F32),
                pltpu.VMEM((total, 128), F32),
            ],
        ),
        compiler_params=params(60),
        cost_estimate=cost(10 * work * 128, 2 * total * 1024, work),
        name="attend_backward",
    )(ids, spots, firsts, where, heads_all, upstream, logs, *tables)


def pull_kernel(
    last, order, every, g_ref, h_ref, w_ref, gain_ref, x_ref, y_ref, gm_ref, hm_ref, w_in_ref, n_in_ref,
    out_ref, w_out_ref, n_out_ref, acc_w,
):
    step = pl.program_id(0)

    @pl.when(step == 0)
    def _():
        acc_w[...] = w_in_ref[...]
        n_out_ref[...] = n_in_ref[...]

    grads = jnp.concatenate([g_ref[...], h_ref[...]], 0)
    grad_mid = jnp.concatenate([gm_ref[...], hm_ref[...]], 0).astype(F32)
    grad_normed = dot(grads, w_ref[...], 1, 1)
    x_f = jnp.concatenate([x_ref[...], y_ref[...]], 0).astype(F32)
    factor = lax.rsqrt(jnp.mean(x_f * x_f, axis=1, keepdims=True) + EPSILON)
    scaled = x_f * factor
    normed = (scaled * gain_ref[...]).astype(BF)
    acc_w[...] += dot(normed, grads, 0, 0)
    n_out_ref[...] += jnp.broadcast_to(
        jnp.sum(grad_normed * scaled, axis=0, keepdims=True), n_out_ref.shape
    )
    inner = grad_normed * gain_ref[...]
    grad_x = factor * (inner - scaled * jnp.mean(inner * scaled, axis=1, keepdims=True))
    out_ref[...] = (grad_x + grad_mid).astype(BF)

    @pl.when(step == pl.num_programs(0) - 1)
    def _():
        if last:
            tail = acc_w[:, 128:]
            acc_w[:, 128:] = jnp.where(lanes_of(tail) == HD, column_of(n_out_ref), tail)
            places = every.shape[0]
            size = acc_w.shape[0] // places
            for j in range(places):
                first = pl.multiple_of(every[j] * size, size)
                w_out_ref[j * size : (j + 1) * size, :] = acc_w[pl.ds(first, size), :].astype(BF)
        else:
            w_out_ref[...] = acc_w[...]


def pull_heads(
    own_grads, w_head, gain, hidden, grad_mid, w_in, n_in, order, every, count, last
):
    total = hidden.shape[0] // 2

    def at(width, j):
        return pl.BlockSpec((count, width), lambda i, order, _: (order[2 * i + j], 0))

    block = pl.BlockSpec((2 * count, D), lambda i, *_: (i, 0))
    return pl.pallas_call(
        functools.partial(pull_kernel, last),
        out_shape=(
            jax.ShapeDtypeStruct((total, D), BF),
            jax.ShapeDtypeStruct((D, 256), BF if last else F32),
            jax.ShapeDtypeStruct((8, D), F32),
        ),
        grid_spec=pltpu.PrefetchScalarGridSpec(
            num_scalar_prefetch=2,
            grid=(total // count // 2,),
            in_specs=[
                at(256, 0), at(256, 1), fixed((D, 256)), fixed((1, D)), at(D, 0), at(D, 1), at(D, 0),
                at(D, 1),
                fixed((D, 256)), fixed((8, D)),
            ],
            out_specs=(block, fixed((D, 256)), fixed((8, D))),
            scratch_shapes=[pltpu.VMEM((D, 256), F32)],
        ),
        compiler_params=params(),
        cost_estimate=cost(4 * total * D * 256, 6 * total * D, weight=1),
        name="pull_last" if last else "pull_first",
    )(
        order, every, own_grads, own_grads, w_head, gain, hidden, hidden, grad_mid, grad_mid, w_in, n_in
    )


def finish_kernel(places, *refs):
    q_ref, k_ref, v_ref, gain_ref, scr = refs[4:]
    for j in range(16):
        scr[places[j]] = refs[j // 4][j % 4].astype(F32)
    total = jnp.zeros_like(scr[0])
    for quad in range(H // 4):
        heads = [scr[4 * quad + j] for j in range(4)]
        for j in range(2):
            first = (4 * quad + 2 * j) * HD
            q_ref[:, first : first + 128] = jnp.concatenate(
                [heads[2 * j][:, :HD], heads[2 * j + 1][:, :HD]], 1
            )
        pairs = [heads[0] + heads[1], heads[2] + heads[3]]
        total = total + pairs[0] + pairs[1]
        for ref, low in ((k_ref, HD), (v_ref, 2 * HD)):
            ref[:, quad * 128 : (quad + 1) * 128] = jnp.concatenate(
                [pair[:, low : low + HD] for pair in pairs], 1
            )
    gain_ref[...] = total[:, 128:]


def finish_heads(places, pieces):
    rows = pieces[0].shape[1]
    shapes = ((rows, D), (rows, D // 2), (rows, D // 2), (rows, 128))
    return pl.pallas_call(
        finish_kernel,
        out_shape=tuple(jax.ShapeDtypeStruct(shape, F32) for shape in shapes),
        grid_spec=pltpu.PrefetchScalarGridSpec(
            num_scalar_prefetch=1,
            grid=(1,),
            in_specs=[fixed(piece.shape) for piece in pieces],
            out_specs=tuple(fixed(shape) for shape in shapes),
            scratch_shapes=[pltpu.VMEM((16, rows, 256), F32)],
        ),
        compiler_params=params(),
        cost_estimate=cost(1, 2**20),
        name="finish_heads",
    )(places, *pieces)


def finish_kernel_experts(in_ref, up_ref, down_ref, tail_ref):
    many = in_ref.shape[0]
    wide, narrow = up_ref.shape[1] // many, down_ref.shape[1] // many
    for j in range(many):
        up_ref[:, j * wide : (j + 1) * wide] = in_ref[j, :, :wide].astype(F32)
        down_ref[:, j * narrow : (j + 1) * narrow] = in_ref[j, :, wide + 128 :].astype(F32)

    @pl.when(pl.program_id(0) == 0)
    def _():
        tail_ref[...] = jnp.zeros_like(tail_ref)

    for j in range(many):
        tail_ref[...] += in_ref[j, :, wide : wide + 128].astype(F32)


def finish_experts(arrived):
    places, rows, width = arrived.shape
    part = (width - 128) // 3
    return pl.pallas_call(
        finish_kernel_experts,
        out_shape=(
            jax.ShapeDtypeStruct((rows, places * 2 * part), F32),
            jax.ShapeDtypeStruct((rows, places * part), F32),
            jax.ShapeDtypeStruct((rows, 128), F32),
        ),
        grid=(places // 4,),
        in_specs=[pl.BlockSpec((4, rows, width), lambda i: (i, 0, 0))],
        out_specs=(
            pl.BlockSpec((rows, 8 * part), lambda i: (0, i)),
            pl.BlockSpec((rows, 4 * part), lambda i: (0, i)),
            fixed((rows, 128)),
        ),
        compiler_params=params(),
        cost_estimate=cost(1, 5 * 2**20),
        name="finish_experts",
    )(arrived)


def per_device(
    hidden_in,
    out_grad,
    doc_lengths,
    block_order,
    routes,
    attn_norm,
    w_query,
    w_key,
    w_value,
    w_output,
    ffn_norm,
    w_router,
    w_gate_up,
    w_down,
):
    ctx_count = lax.axis_size("ctx")
    ctx_place = lax.axis_index("ctx")
    fsdp_place = lax.axis_index("fsdp")
    copies = ctx_count // E
    own_expert, own_copy = ctx_place // copies, ctx_place % copies
    tok_count = hidden_in.shape[1]
    seq_len = tok_count * ctx_count
    block_len = tok_count // 2
    band = seq_len // 4
    rows = attn_norm.shape[0]
    part = F // copies
    groups = H // KVH
    share = seq_len // copies
    swap_y = [(0, 1), (1, 0)]
    alone = copies == 1

    def swap_fsdp(mine):
        return lax.ppermute(mine, "fsdp", swap_y)

    def both_rows(mine):
        theirs = swap_fsdp(mine)
        stacked = jnp.where(
            fsdp_place == 0, jnp.stack([mine, theirs], 1), jnp.stack([theirs, mine], 1)
        )
        return stacked.reshape(-1, mine.shape[-1])

    def exchange(split):
        return lax.all_to_all(split, "ctx", 0, 0, tiled=True)

    ids = block_order[0]
    block_ids = jnp.arange(ids.shape[0], dtype=jnp.int32)
    spots = jnp.sum(jnp.where(ids[None, :] == block_ids[:, None], block_ids[None, :], 0), axis=1)
    lengths = doc_lengths[0]
    doc_ids = jnp.arange(lengths.shape[0], dtype=jnp.int32)
    firsts = jnp.sum(
        jnp.where(doc_ids[None, :] < doc_ids[:, None], lengths[None, :], 0), axis=1
    )
    tables = tables_of(seq_len)
    order, heads = block_order_of(ctx_count), block_order_of(E)
    where = jnp.stack([own_expert, own_copy, ctx_place, jnp.int32(share)]).astype(jnp.int32)

    def by_expert(weight, pieces):
        split = weight.reshape(rows, E, pieces, copies, part)
        return split.transpose(1, 3, 0, 2, 4).reshape(ctx_count, rows, pieces * part)

    chosen_mask = jnp.any(
        routes[0][:, :, None] == jnp.arange(E, dtype=jnp.int32)[None, None, :], axis=1
    ).astype(BF)
    grads_own = jnp.concatenate(
        [out_grad[0], chosen_mask, jnp.zeros((tok_count, 128 - E), BF)], axis=1
    )
    experts = jnp.concatenate([by_expert(w_gate_up, 2), by_expert(w_down, 1)], axis=2)
    norms = jnp.stack([attn_norm, ffn_norm], 1)
    if alone:
        small_here = exchange(pack_small(copies, w_query, w_key, w_value, w_router, norms))
        w_ext, w_head, router_full, gain_one, gain_two = split_small(both_rows(small_here))
        near = Gather(hidden_in[0])
        near.cross()
        near.last(small_here)
        experts_here = exchange(after(experts, near.two))
        hidden_all = near.join(order, "join_hidden", w_ext).reshape(seq_len, D)
    else:
        small_here = exchange(pack_small(copies, w_query, w_key, w_value, w_router, norms))
        w_ext, w_head, router_full, gain_one, gain_two = split_small(both_rows(small_here))
        hidden_all = lax.all_gather(hidden_in[0], "ctx", axis=0, tiled=True)
        experts_here = exchange(experts)
    out_all = lax.all_gather(w_output, BOTH, axis=0, tiled=True).reshape(ctx_count, 2 * rows, D)
    top_all = lax.all_gather(grads_own[None], "ctx", axis=0, tiled=True)

    heads_all, logs, attended = head_forward(
        hidden_all, w_ext, gain_one, tables, ids, spots, firsts, tok_count, band
    )
    def half_rows(mine, theirs):
        stacked = jnp.where(
            fsdp_place == 0, jnp.stack([mine, theirs], 1), jnp.stack([theirs, mine], 1)
        )
        return stacked.reshape(D, mine.shape[-1])

    if alone:
        att = Gather(attended)
        experts_here = after(experts_here, att.one, att.three)
    gu_here, dn_here = experts_here[:, :, : 2 * part], experts_here[:, :, 2 * part :]
    gu_there, dn_there = swap_fsdp(gu_here), swap_fsdp(dn_here)
    w_gu, w_dn = half_rows(gu_here, gu_there), half_rows(dn_here, dn_there)
    if alone:
        att.cross()
        att.last(experts_here)
        att_all = att.join(heads, "join_heads", w_gu)
    else:
        sent = lax.dynamic_slice_in_dim(attended, own_copy * share, share, 1)
        att_all = lax.all_gather(sent, "ctx", axis=0, tiled=True)
        att_all = att_all.reshape(H, copies, HD, share).transpose(0, 2, 1, 3)
        att_all = att_all.reshape(H, HD, seq_len)

    act, grad_mid, pull_a, pull_b, grads_expert, middle = expert_main(
        att_all, hidden_all, top_all, out_all, w_gu, w_dn, router_full, gain_two, heads, where,
        tok_count,
    )

    def given_rows(grads):
        by_owner = grads.reshape(ctx_count, 2, rows, grads.shape[1])
        return by_owner, lax.dynamic_index_in_dim(by_owner, 1 - fsdp_place, 1, keepdims=False)

    def to_owner(by_owner, theirs):
        kept = lax.dynamic_index_in_dim(by_owner, fsdp_place, 1, keepdims=False)
        return (kept.astype(F32) + theirs.astype(F32)).astype(BF)

    owner, given = given_rows(grads_expert)
    theirs = swap_fsdp(given)
    mid_late = grad_mid
    if alone:
        ring = RingSum(pull_a, permute(pull_b, SWAP_CORE))
        mid_late = after(grad_mid, ring.cross_out)
    moe = moe_out(act, w_dn, tok_count, rows)
    out_both = output_weights(
        att_all, mid_late, top_all, moe, where, tok_count, rows
    )
    if alone:
        ring.cross()
        out_both = after(out_both, *ring.sends)
    if alone:
        upstream = ring.end(theirs)
    else:
        joined = jnp.concatenate([pull_a, pull_b], 0)
        pulled = lax.psum_scatter(joined, "ctx", scatter_dimension=0, tiled=True)
        rings = [[i * copies + j for j in range(copies)] for i in range(E)]
        pulled = lax.all_gather(pulled, "ctx", axis=0, tiled=True, axis_index_groups=rings)
        own_out = lax.dynamic_slice_in_dim(out_all.reshape(D, D), own_expert * HD, HD, 0)
        top_rows = top_all[:, :, :D].reshape(seq_len, D)
        upstream = pulled.astype(F32) + RESIDUAL_SCALE * dot(own_out, top_rows, 1, 1)
    if alone:
        theirs = after(theirs, upstream)
    grads_all_expert = to_owner(owner, theirs)

    own_grads = attend_backward(
        heads_all, upstream, logs, tables, ids, spots, firsts, where, tok_count, band
    )
    experts_in = exchange(grads_all_expert)
    grad_b, head_sum, norm_head = pull_heads(
        own_grads, w_head, gain_one, hidden_all, grad_mid, jnp.zeros((D, 256), F32),
        jnp.zeros((8, D), F32), order[ctx_count // 2 :], order, tok_count, False,
    )
    grad_a, grad_heads, ignored = pull_heads(
        own_grads, w_head, gain_one, hidden_all, grad_mid, head_sum, norm_head,
        order[: ctx_count // 2], order, tok_count, True,
    )
    if alone:
        by_owner = grad_heads.reshape(ctx_count, 2, rows, 256)
        kept = lax.dynamic_index_in_dim(by_owner, fsdp_place, 1, keepdims=False)
        given = lax.dynamic_index_in_dim(by_owner, 1 - fsdp_place, 1, keepdims=False)
        theirs = swap_fsdp(given)
        ring = RingSum(grad_a, permute(grad_b, SWAP_CORE))
        ring.cross()
        theirs = after(theirs, *ring.sends)
        tail_sum = (kept.astype(F32) + theirs.astype(F32)).astype(BF)
        experts_in = after(experts_in, *ring.sends)
    else:
        joined = jnp.concatenate([grad_a, grad_b], 0)
        grad_own = lax.psum_scatter(joined, "ctx", scatter_dimension=0, tiled=True).astype(F32)
    def from_experts(block, pieces):
        block = block[:, :, : pieces * part].astype(F32)
        block = block.reshape(E, copies, rows, pieces, part).transpose(2, 0, 3, 1, 4)
        return block.reshape(rows, E * pieces * F)

    if alone:
        share_gate_up, share_down, tail = finish_experts(experts_in)
    else:
        gu_in = experts_in[:, :, : 2 * part + 128]
        dn_in = experts_in[:, :, 2 * part + 128 :]
        share_gate_up = from_experts(gu_in, 2)
        share_down = from_experts(dn_in, 1)
        tail = jnp.sum(gu_in[:, :, 2 * part :].astype(F32), axis=0)
    share_router = tail[:, :E]
    share_gain_two = tail[:, E]
    out_own = lax.psum_scatter(out_both, "ctx", scatter_dimension=0, tiled=False).astype(F32)
    hidden_out = (middle + out_own[:tok_count]).astype(BF)
    out_rows = out_own[tok_count:].reshape(2, rows, D)
    mine = lax.dynamic_index_in_dim(out_rows, fsdp_place, 0, keepdims=False)
    theirs = lax.dynamic_index_in_dim(out_rows, 1 - fsdp_place, 0, keepdims=False)
    share_output = mine + swap_fsdp(theirs)

    if alone:
        grad_own = ring.end(share_output, hidden_out, share_gate_up)
    grad_in = out_grad[0].astype(F32) + grad_own
    if alone:
        pieces = spread_ctx(tail_sum)
        share_query, share_key, share_value, gain_sum = finish_heads(sender_order_of(), pieces)
        share_gain_one = gain_sum[:, HD]
    else:
        tail_in = lax.all_to_all(
            grad_heads.reshape(2 * ctx_count, rows, 256), BOTH, 0, 0, tiled=True
        )
        tail_in = tail_in.astype(F32).reshape(H, copies * 2, rows, 256)
        heads_in = jnp.sum(tail_in[..., : 3 * HD], axis=1)
        share_query = heads_in[:, :, :HD].transpose(1, 0, 2).reshape(rows, H * HD)
        pairs_in = heads_in[:, :, HD:].reshape(KVH, groups, rows, 2, HD).sum(1)
        share_key = pairs_in[:, :, 0].transpose(1, 0, 2).reshape(rows, KVH * HD)
        share_value = pairs_in[:, :, 1].transpose(1, 0, 2).reshape(rows, KVH * HD)
        share_gain_one = jnp.sum(tail_in[..., 3 * HD], axis=(0, 1))
    return (
        hidden_out[None],
        grad_in[None],
        share_gain_one,
        share_query,
        share_key,
        share_value,
        share_output,
        share_gain_two,
        share_router,
        share_gate_up,
        share_down,
    )


def solution(mesh):
    return jax.shard_map(
        per_device,
        mesh=mesh,
        in_specs=(
            P("fsdp", "ctx", None),
            P("fsdp", "ctx", None),
            P("fsdp", None),
            P("fsdp", None),
            P("fsdp", "ctx", None),
            P(BOTH),
            P(BOTH, None),
            P(BOTH, None),
            P(BOTH, None),
            P(BOTH, None),
            P(BOTH),
            P(BOTH, None),
            P(BOTH, None),
            P(BOTH, None),
        ),
        out_specs=(
            P("fsdp", "ctx", None),
            P("fsdp", "ctx", None),
            P(BOTH),
            P(BOTH, None),
            P(BOTH, None),
            P(BOTH, None),
            P(BOTH, None),
            P(BOTH),
            P(BOTH, None),
            P(BOTH, None),
            P(BOTH, None),
        ),
        check_vma=False,
    )
```

profile of v0, /device:TPU:0, one launch (start us, length us, event | category | flops | bytes accessed | tf_op | source)
XLA Modules:
  0.0 406.4 jit_solution(10609998367462436061)
XLA Ops:
  8.8 1.8 concatenate.27
  10.6 3.1 collective-permute-start.4
  13.7 2.1 collective-permute-start.5
  17.2 1.4 copy.62.wr_ref
  18.5 1.7 pack_small.1
  20.3 4.3 %all-to-all-start = ((bf16[16,32,256]{2,1,0:T(8,128)(2,1)}), bf16[16,32,256]{2,1,0:T(8,128)(2,1)S(1)}, u32[]{:S(2)}, u32[]{:S(2)}) async-start(bf16[16,32,256]{2,1,0:T(8,128)(2,1)} %pack_small.1), calls=%async_computation | async-start | bytes 524288 | tf_op jit(solution)/shard_map/all_to_all | solution.py:865
  24.5 3.2 collective-permute-done.5.refs_6_
  27.8 1.6 collective-permute-start.6
  30.5 5.3 %all-to-all-done = bf16[16,32,256]{2,1,0:T(8,128)(2,1)S(1)} async-done(((bf16[16,32,256]{2,1,0:T(8,128)(2,1)}), bf16[16,32,256]{2,1,0:T(8,128)(2,1)S(1)}, u32[]{:S(2)}, u32[]{:S(2)}) %all-to-all-start) | async-done | bytes 262176 | tf_op jit(solution)/shard_map/all_to_all | solution.py:865
  35.8 1.5 collective-permute-start.3
  37.3 5.7 %collective-permute-start.7 = (bf16[128,1024]{1,0:T(8,128)(2,1)}, bf16[128,1024]{1,0:T(8,128)(2,1)}, u32[]{:S(2)}, u32[]{:S(2)}) collective-permute-start(bf16[128,1024]{1,0:T(8,128)(2,1)} %bitcast.3.refs_0_), channel_id=1, source_target_pairs={{0,2},{2,0},{4,6},{6,4},{8,10},{10,8},{12,14},{14,12},{16,18},{18,... | collective-permute-start | bytes 786440 | tf_op jit(solution)/shard_map/ppermute | solution.py:37
  43.6 2.8 collective-permute-done.1.refs_4_
  46.4 1.5 collective-permute-start.2
  53.3 2.4 split_weights.1
  58.2 6.4 %all-to-all-start.1 = ((bf16[16,32,1536]{2,1,0:T(8,128)(2,1)}), bf16[16,32,1536]{2,1,0:T(8,128)(2,1)S(1)}, u32[]{:S(2)}, u32[]{:S(2)}) async-start(bf16[16,32,1536]{2,1,0:T(8,128)(2,1)} %pad_maximum_fusion), calls=%async_computation.1 | async-start | bytes 3145728 | tf_op jit(solution)/shard_map/all_to_all | solution.py:865
  65.6 5.0 %join_hidden.1 = bf16[16,128,1024]{2,1,0:T(8,128)(2,1)} custom-call(s32[16]{0:T(128)} %fusion.13.places.heads.every, bf16[128,1024]{1,0:T(8,128)(2,1)} %bitcast.3.refs_0_, bf16[128,1024]{1,0:T(8,128)(2,1)} %collective-permute-done.refs_1_, bf16[128,1024]{1,0:T(8,128)(2,1)} %copy-done.6, bf16[256,1024]{1,0:T(8,128)(2,1)} %copy-done.10, ...), custom_call_target="tpu_custom_call" | custom-call | flops 20 | bytes 167772160 | tf_op jit(solution)/shard_map/join_hidden/pallas_call | solution.py:151
  70.5 18.4 %head_forward.1 = (bf16[2048,512]{1,0:T(8,128)(2,1)}, f32[2048,1]{1,0:T(8,128)}, bf16[64,2048]{1,0:T(8,128)(2,1)}) custom-call(s32[32]{0:T(128)} %bitcast.120, s32[32]{0:T(128)} %select_reduce_fusion.spots, s32[16]{0:T(128)} %select_reduce_fusion.1.firsts, bf16[2048,1024]{1,0:T(8,128)(2,1)} %bitcast.82, bf16[1024,384]{1,0:T(8,128)(2,1)} %get-tuple-element.53.w_ref, ...), custom_call_target="tpu_custom_call" | custom-call | flops 32212254720 | bytes 83886080 | tf_op jit(solution)/shard_map/head_forward/pallas_call | solution.py:352
  89.0 1.9 collective-permute-start.16
  90.9 2.1 collective-permute-start.17
  93.0 15.9 %collective-permute-done.16.refs_2_ = bf16[64,2048]{1,0:T(8,128)(2,1)S(1)} collective-permute-done((bf16[64,2048]{1,0:T(8,128)(2,1)}, bf16[64,2048]{1,0:T(8,128)(2,1)S(1)}, u32[]{:S(2)}, u32[]{:S(2)}) %collective-permute-start.16) | collective-permute-done | bytes 262176 | tf_op jit(solution)/shard_map/ppermute | solution.py:37
  108.9 6.1 %collective-permute-done.17.refs_6_ = bf16[64,2048]{1,0:T(8,128)(2,1)S(1)} collective-permute-done((bf16[64,2048]{1,0:T(8,128)(2,1)}, bf16[64,2048]{1,0:T(8,128)(2,1)S(1)}, u32[]{:S(2)}, u32[]{:S(2)}) %collective-permute-start.17) | collective-permute-done | bytes 262176 | tf_op jit(solution)/shard_map/ppermute | solution.py:37
  115.3 2.1 collective-permute-start.19
  117.4 6.4 %collective-permute-start.20 = (bf16[128,2048]{1,0:T(8,128)(2,1)S(1)}, bf16[128,2048]{1,0:T(8,128)(2,1)S(1)}, u32[]{:S(2)}, u32[]{:S(2)}) collective-permute-start(bf16[128,2048]{1,0:T(8,128)(2,1)S(1)} %pad_maximum_fusion.4), channel_id=1, source_target_pairs={{0,4},{2,6},{4,0},{6,2},{8,12},{10,14},{12,8},{14,10},{16,20},{18,... | collective-permute-start | bytes 1572872 | tf_op jit(solution)/shard_map/ppermute | solution.py:37
  123.8 7.0 %collective-permute-start.15 = (bf16[64,2048]{1,0:T(8,128)(2,1)S(1)}, bf16[64,2048]{1,0:T(8,128)(2,1)}, u32[]{:S(2)}, u32[]{:S(2)}) collective-permute-start(bf16[64,2048]{1,0:T(8,128)(2,1)S(1)} %copy-done.16), channel_id=1, source_target_pairs={{0,16},{2,18},{4,20},{6,22},{8,24},{10,26},{12,28},{14,30},{16,0},... | collective-permute-start | bytes 786440 | tf_op jit(solution)/shard_map/ppermute | solution.py:37
  132.0 22.5 %collective-permute-done.15.refs_4_ = bf16[64,2048]{1,0:T(8,128)(2,1)} collective-permute-done((bf16[64,2048]{1,0:T(8,128)(2,1)S(1)}, bf16[64,2048]{1,0:T(8,128)(2,1)}, u32[]{:S(2)}, u32[]{:S(2)}) %collective-permute-start.15) | collective-permute-done | bytes 262176 | tf_op jit(solution)/shard_map/ppermute | solution.py:37
  156.0 1.6 copy.67
  157.6 3.9 collective-permute-done.18.refs_5_
  165.6 4.9 %join_heads.1.att_ref = bf16[16,64,2048]{2,1,0:T(8,128)(2,1)} custom-call(s32[16]{0:T(128)} %fusion.13.places.heads.every, bf16[64,2048]{1,0:T(8,128)(2,1)} %get-tuple-element.57.refs_0_, bf16[64,2048]{1,0:T(8,128)(2,1)} %collective-permute-done.14.refs_1_, bf16[64,2048]{1,0:T(8,128)(2,1)} %copy-done.8, bf16[128,2048]{1,0:T(8,128)(2,1)} %copy-done.11, ...), custom_call_target="tpu_custom_call" | custom-call | flops 20 | bytes 167772160 | tf_op jit(solution)/shard_map/join_heads/pallas_call | solution.py:151
  170.5 49.9 %expert_main.1 = (bf16[2048,512]{1,0:T(8,128)(2,1)}, bf16[2048,1024]{1,0:T(8,128)(2,1)}, bf16[512,2048]{1,0:T(8,128)(2,1)}, bf16[512,2048]{1,0:T(8,128)(2,1)}, b...) custom-call(s32[16]{0:T(128)} %fusion.13.places.heads.every, s32[4]{0:T(128)} %pad_add_fusion.where, ...), custom_call_target="tpu_custom_call" | custom-call | flops 51539607552 | bytes 50331648 | tf_op jit(solution)/shard_map/expert_main/pallas_call | solution.py:490
  221.0 2.8 dynamic-slice_bitcast_fusion
  223.8 6.3 %moe_out.1.moe_ref = bf16[16,192,1024]{2,1,0:T(8,128)(2,1)} custom-call(bf16[2048,512]{1,0:T(8,128)(2,1)} %get-tuple-element.70.act_ref, bf16[1024,512]{1,0:T(8,128)(2,1)} %bitcast.97), custom_call_target="tpu_custom_call" | custom-call | flops 42949672960 | bytes 125829120 | tf_op jit(solution)/shard_map/moe_out/pallas_call | solution.py:533
  232.0 10.9 %output_weights.1 = bf16[16,192,1024]{2,1,0:T(8,128)(2,1)} custom-call(s32[4]{0:T(128)} %pad_add_fusion.where, bf16[16,64,2048]{2,1,0:T(8,128)(2,1)} %join_heads.1.att_ref, bf16[2048,1024]{1,0:T(8,128)(2,1)} %get-tuple-element.69.v_ref.gm_ref.hm_ref, bf16[16,128,1152]{2,1,0:T(8,128)(2,1)} %bitcast.115, ...), custom_call_target="tpu_custom_call", output_to_operand_aliasing={{}: (4, {})} | custom-call | flops 85899345920 | bytes 335544320 | tf_op jit(solution)/shard_map/output_weights/pallas_call | solution.py:569
  242.9 8.4 %collective-permute-done.30 = bf16[192,2048]{1,0:T(8,128)(2,1)} collective-permute-done((bf16[192,2048]{1,0:T(8,128)(2,1)S(1)}, bf16[192,2048]{1,0:T(8,128)(2,1)}, u32[]{:S(2)}, u32[]{:S(2)}) %collective-permute-start.30) | collective-permute-done | bytes 786464 | tf_op jit(solution)/shard_map/ppermute | solution.py:37
  251.3 1.9 add_convert_fusion.8
  253.3 5.3 %collective-permute-start.32 = (bf16[64,2048]{1,0:T(8,128)(2,1)S(1)}, bf16[64,2048]{1,0:T(8,128)(2,1)S(1)}, u32[]{:S(2)}, u32[]{:S(2)}) collective-permute-start(bf16[64,2048]{1,0:T(8,128)(2,1)S(1)} %get-tuple-element.142), channel_id=1, source_target_pairs={{0,16},{2,18},{4,20},{6,22},{8,24},{10,26},{12,28},{14,30},{16,0},... | collective-permute-start | bytes 786440 | tf_op jit(solution)/shard_map/ppermute | solution.py:37
  258.6 1.4 collective-permute-start.31
  260.0 2.2 collective-permute-start.34
  263.2 10.3 %collective-permute-done.32 = bf16[64,2048]{1,0:T(8,128)(2,1)S(1)} collective-permute-done((bf16[64,2048]{1,0:T(8,128)(2,1)S(1)}, bf16[64,2048]{1,0:T(8,128)(2,1)S(1)}, u32[]{:S(2)}, u32[]{:S(2)}) %collective-permute-start.32) | collective-permute-done | bytes 262176 | tf_op jit(solution)/shard_map/ppermute | solution.py:37
  273.5 3.7 collective-permute-done.35
  277.2 2.0 convert_add_fusion.2.up_ref
  279.2 15.8 %attend_backward.1.g_ref.h_ref = bf16[2048,256]{1,0:T(8,128)(2,1)} custom-call(s32[32]{0:T(128)} %bitcast.121, s32[32]{0:T(128)} %select_reduce_fusion.spots, s32[16]{0:T(128)} %select_reduce_fusion.1.firsts, s32[4]{0:T(128)} %pad_add_fusion.where, bf16[2048,512]{1,0:T(8,128)(2,1)} %get-tuple-element.72.all_ref, f32[64,2048]{1,0:T(8,128)} %convert_add_fusion.2.up_ref, ...), custom_call_target="tpu_custom_call" | custom-call | flops 40265318400 | bytes 83886080 | tf_op jit(solution)/shard_map/attend_backward/pallas_call | solution.py:646
  296.6 8.1 %pull_first.1 = (bf16[1024,1024]{1,0:T(8,128)(2,1)}, f32[1024,256]{1,0:T(8,128)}, f32[8,1024]{1,0:T(8,128)}) custom-call(s32[8]{0:T(128)} %get-tuple-element.164.order, s32[16]{0:T(128)} %fusion.13.places.heads.every, bf16[2048,256]{1,0:T(8,128)(2,1)} %attend_backward.1.g_ref.h_ref, bf16[2048,256]{1,0:T(8,128)(2,1)} %attend_backward.1.g_ref.h_ref, ...), custom_call_target="tpu_custom_call" | custom-call | flops 1073741824 | bytes 6291456 | tf_op jit(solution)/shard_map/pull_first/pallas_call | solution.py:718
  304.8 3.1 fusion
  307.9 7.2 %all-to-all-start.2 = ((bf16[16,32,1664]{2,1,0:T(8,128)(2,1)}), bf16[16,32,1664]{2,1,0:T(8,128)(2,1)S(1)}, u32[]{:S(2)}, u32[]{:S(2)}) async-start(bf16[16,32,1664]{2,1,0:T(8,128)(2,1)} %fusion), calls=%async_computation.3 | async-start | bytes 3407872 | tf_op jit(solution)/shard_map/all_to_all | solution.py:865
  315.1 7.9 %pull_last.1 = (bf16[1024,1024]{1,0:T(8,128)(2,1)}, bf16[1024,256]{1,0:T(8,128)(2,1)}, f32[8,1024]{1,0:T(8,128)}) custom-call(s32[8]{0:T(128)} %get-tuple-element.163.order, s32[16]{0:T(128)} %fusion.13.places.heads.every, bf16[2048,256]{1,0:T(8,128)(2,1)} %attend_backward.1.g_ref.h_ref, bf16[2048,256]{1,0:T(8,128)(2,1)} %attend_backward.1.g_ref.h_ref, ...), custom_call_target="tpu_custom_call" | custom-call | flops 1073741824 | bytes 6291456 | tf_op jit(solution)/shard_map/pull_last/pallas_call | solution.py:718
  323.0 1.9 add_convert_fusion.6
  325.1 2.0 collective-permute-start.38
  327.8 28.0 %collective-permute-done.38 = bf16[384,1024]{1,0:T(8,128)(2,1)S(1)} collective-permute-done((bf16[384,1024]{1,0:T(8,128)(2,1)S(1)}, bf16[384,1024]{1,0:T(8,128)(2,1)S(1)}, u32[]{:S(2)}, u32[]{:S(2)}) %collective-permute-start.38) | collective-permute-done | bytes 786464 | tf_op jit(solution)/shard_map/ppermute | solution.py:37
  355.8 1.8 add_convert_fusion.2
  359.2 2.5 collective-permute-start.45
  362.3 2.5 collective-permute-start.39
  364.7 1.5 collective-permute-done.45
  366.9 2.9 collective-permute-start.46
  369.8 2.9 collective-permute-start.47
  374.0 3.9 finish_experts.1
  377.9 1.4 copy.73
  379.3 1.4 slice_reduce_fusion
  380.7 3.8 collective-permute-start.41
  384.5 1.4 collective-permute-done.47.refs_2_
  385.9 2.4 finish_heads.1
  388.3 1.4 slice_reduce_fusion.1
  390.7 1.5 collective-permute-start.40
  394.1 1.9 collective-permute-done.40
  397.6 2.2 add_bitcast_fusion
  (180 shorter events, 35.0 us)
Async XLA Ops:
  7.2 35.8 %copy-start.29 = (s32[1,16]{1,0:T(1,128)S(1)}, s32[1,16]{1,0:T(1,128)}, u32[]{:S(2)}) copy-start(s32[1,16]{1,0:T(1,128)} %param.18) | copy-start | bytes 196
  7.2 41.5 %copy-start.5 = (bf16[32,16384]{1,0:T(8,128)(2,1)S(1)}, bf16[32,16384]{1,0:T(8,128)(2,1)}, u32[]{:S(2)}) copy-start(bf16[32,16384]{1,0:T(8,128)(2,1)} %param.28) | copy-start | bytes 3145732
  7.2 163.3 %all-gather.4.cloned.1.call-start = ((), (), s32[]{:S(2)}) async-start(), calls=%async_computation.4 | async-start | bytes 2162688 | tf_op jit(solution)/shard_map/all_gather | solution.py:904
  7.9 162.6 %all-gather.6.cloned.1.call-start = ((), (), s32[]{:S(2)}) async-start(), calls=%async_computation.6 | async-start | bytes 5013504 | tf_op jit(solution)/shard_map/all_gather | solution.py:905
  10.6 13.9 %collective-permute-start.4 = (bf16[128,1024]{1,0:T(8,128)(2,1)}, bf16[128,1024]{1,0:T(8,128)(2,1)S(1)}, u32[]{:S(2)}, u32[]{:S(2)}) collective-permute-start(bf16[128,1024]{1,0:T(8,128)(2,1)} %bitcast.3.refs_0_), channel_id=1, source_target_pairs={{0,8},{2,10},{4,12},{6,14},{8,16},{10,18},{12,20},{14,22},{16,24},... | collective-permute-start | bytes 786440 | tf_op jit(solution)/shard_map/ppermute | solution.py:37
  13.7 14.1 %collective-permute-start.5 = (bf16[128,1024]{1,0:T(8,128)(2,1)}, bf16[128,1024]{1,0:T(8,128)(2,1)S(1)}, u32[]{:S(2)}, u32[]{:S(2)}) collective-permute-start(bf16[128,1024]{1,0:T(8,128)(2,1)} %bitcast.3.refs_0_), channel_id=1, source_target_pairs={{0,24},{2,26},{4,28},{6,30},{8,0},{10,2},{12,4},{14,6},{16,8},{18,... | collective-permute-start | bytes 786440 | tf_op jit(solution)/shard_map/ppermute | solution.py:37
  20.3 15.6 %all-to-all-start = ((bf16[16,32,256]{2,1,0:T(8,128)(2,1)}), bf16[16,32,256]{2,1,0:T(8,128)(2,1)S(1)}, u32[]{:S(2)}, u32[]{:S(2)}) async-start(bf16[16,32,256]{2,1,0:T(8,128)(2,1)} %pack_small.1), calls=%async_computation | async-start | bytes 524288 | tf_op jit(solution)/shard_map/all_to_all | solution.py:865
  24.5 31.2 %copy-start.6 = (bf16[128,1024]{1,0:T(8,128)(2,1)}, bf16[128,1024]{1,0:T(8,128)(2,1)S(1)}, u32[]{:S(2)}) copy-start(bf16[128,1024]{1,0:T(8,128)(2,1)S(1)} %collective-permute-done.4.refs_2_) | copy-start | bytes 786436
  27.8 22.5 %copy-start.7 = (bf16[128,1024]{1,0:T(8,128)(2,1)}, bf16[128,1024]{1,0:T(8,128)(2,1)S(1)}, u32[]{:S(2)}) copy-start(bf16[128,1024]{1,0:T(8,128)(2,1)S(1)} %collective-permute-done.5.refs_6_) | copy-start | bytes 786436
  27.8 20.2 %collective-permute-start.6 = (bf16[256,1024]{1,0:T(8,128)(2,1)S(1)}, bf16[256,1024]{1,0:T(8,128)(2,1)S(1)}, u32[]{:S(2)}, u32[]{:S(2)}) collective-permute-start(bf16[256,1024]{1,0:T(8,128)(2,1)S(1)} %pad_maximum_fusion.3), channel_id=1, source_target_pairs={{0,4},{2,6},{4,0},{6,2},{8,12},{10,14},{12,8},{14,10},{16,20},{18,... | collective-permute-start | bytes 1572872 | tf_op jit(solution)/shard_map/ppermute | solution.py:37
  29.4 17.1 %collective-permute-start.1 = (bf16[128,1024]{1,0:T(8,128)(2,1)}, bf16[128,1024]{1,0:T(8,128)(2,1)}, u32[]{:S(2)}, u32[]{:S(2)}) collective-permute-start(bf16[128,1024]{1,0:T(8,128)(2,1)} %bitcast.3.refs_0_), channel_id=1, source_target_pairs={{0,16},{2,18},{4,20},{6,22},{8,24},{10,26},{12,28},{14,30},{16,0},... | collective-permute-start | bytes 786440 | tf_op jit(solution)/shard_map/ppermute | solution.py:37
  35.8 10.6 %collective-permute-start.3 = (bf16[16,32,256]{2,1,0:T(8,128)(2,1)S(1)}, bf16[16,32,256]{2,1,0:T(8,128)(2,1)S(1)}, u32[]{:S(2)}, u32[]{:S(2)}) collective-permute-start(bf16[16,32,256]{2,1,0:T(8,128)(2,1)S(1)} %all-to-all-done), channel_id=1, source_target_pairs={{0,1},{1,0},{2,3},{3,2},{4,5},{5,4},{6,7},{7,6},{8,9},{9,8},{10,11... | collective-permute-start | bytes 786440 | tf_op jit(solution)/shard_map/ppermute | solution.py:855
  37.3 18.5 %collective-permute-start = (bf16[128,1024]{1,0:T(8,128)(2,1)}, bf16[128,1024]{1,0:T(8,128)(2,1)}, u32[]{:S(2)}, u32[]{:S(2)}) collective-permute-start(bf16[128,1024]{1,0:T(8,128)(2,1)} %bitcast.3.refs_0_), channel_id=1, source_target_pairs={{0,4},{2,6},{4,0},{6,2},{8,12},{10,14},{12,8},{14,10},{16,20},{18,... | collective-permute-start | bytes 786440 | tf_op jit(solution)/shard_map/ppermute | solution.py:37
  37.3 19.1 %collective-permute-start.7 = (bf16[128,1024]{1,0:T(8,128)(2,1)}, bf16[128,1024]{1,0:T(8,128)(2,1)}, u32[]{:S(2)}, u32[]{:S(2)}) collective-permute-start(bf16[128,1024]{1,0:T(8,128)(2,1)} %bitcast.3.refs_0_), channel_id=1, source_target_pairs={{0,2},{2,0},{4,6},{6,4},{8,10},{10,8},{12,14},{14,12},{16,18},{18,... | collective-permute-start | bytes 786440 | tf_op jit(solution)/shard_map/ppermute | solution.py:37
  46.4 10.3 %collective-permute-start.13 = (bf16[128,1024]{1,0:T(8,128)(2,1)S(1)}, bf16[128,1024]{1,0:T(8,128)(2,1)}, u32[]{:S(2)}, u32[]{:S(2)}) collective-permute-start(bf16[128,1024]{1,0:T(8,128)(2,1)S(1)} %collective-permute-done.5.refs_6_), channel_id=1, source_target_pairs={{0,2},{2,0},{4,6},{6,4},{8,10},{10,8},{12,14},{14,12},{16,18},{18,... | collective-permute-start | bytes 786440 | tf_op jit(solution)/shard_map/ppermute | solution.py:37
  46.4 9.7 %collective-permute-start.2 = (bf16[128,1024]{1,0:T(8,128)(2,1)}, bf16[128,1024]{1,0:T(8,128)(2,1)}, u32[]{:S(2)}, u32[]{:S(2)}) collective-permute-start(bf16[128,1024]{1,0:T(8,128)(2,1)} %collective-permute-done.1.refs_4_), channel_id=1, source_target_pairs={{0,4},{2,6},{4,0},{6,2},{8,12},{10,14},{12,8},{14,10},{16,20},{18,... | collective-permute-start | bytes 786440 | tf_op jit(solution)/shard_map/ppermute | solution.py:37
  48.0 16.7 %collective-permute-start.10 = (bf16[256,1024]{1,0:T(8,128)(2,1)S(1)}, bf16[256,1024]{1,0:T(8,128)(2,1)}, u32[]{:S(2)}, u32[]{:S(2)}) collective-permute-start(bf16[256,1024]{1,0:T(8,128)(2,1)S(1)} %collective-permute-done.6.refs_3_), channel_id=1, source_target_pairs={{0,2},{2,0},{4,6},{6,4},{8,10},{10,8},{12,14},{14,12},{16,18},{18,... | collective-permute-start | bytes 1572872 | tf_op jit(solution)/shard_map/ppermute | solution.py:37
  55.8 8.8 %collective-permute-start.9 = (bf16[128,1024]{1,0:T(8,128)(2,1)S(1)}, bf16[128,1024]{1,0:T(8,128)(2,1)S(1)}, u32[]{:S(2)}, u32[]{:S(2)}) collective-permute-start(bf16[128,1024]{1,0:T(8,128)(2,1)S(1)} %collective-permute-done.4.refs_2_), channel_id=1, source_target_pairs={{0,2},{2,0},{4,6},{6,4},{8,10},{10,8},{12,14},{14,12},{16,18},{18,... | collective-permute-start | bytes 786440 | tf_op jit(solution)/shard_map/ppermute | solution.py:37
  56.2 8.4 %collective-permute-start.11 = (bf16[128,1024]{1,0:T(8,128)(2,1)}, bf16[128,1024]{1,0:T(8,128)(2,1)S(1)}, u32[]{:S(2)}, u32[]{:S(2)}) collective-permute-start(bf16[128,1024]{1,0:T(8,128)(2,1)} %collective-permute-done.1.refs_4_), channel_id=1, source_target_pairs={{0,2},{2,0},{4,6},{6,4},{8,10},{10,8},{12,14},{14,12},{16,18},{18,... | collective-permute-start | bytes 786440 | tf_op jit(solution)/shard_map/ppermute | solution.py:37
  56.4 8.3 %collective-permute-start.12 = (bf16[128,1024]{1,0:T(8,128)(2,1)}, bf16[128,1024]{1,0:T(8,128)(2,1)S(1)}, u32[]{:S(2)}, u32[]{:S(2)}) collective-permute-start(bf16[128,1024]{1,0:T(8,128)(2,1)} %collective-permute-done.2.refs_5_), channel_id=1, source_target_pairs={{0,2},{2,0},{4,6},{6,4},{8,10},{10,8},{12,14},{14,12},{16,18},{18,... | collective-permute-start | bytes 786440 | tf_op jit(solution)/shard_map/ppermute | solution.py:37
  56.7 8.0 %collective-permute-start.8 = (bf16[128,1024]{1,0:T(8,128)(2,1)}, bf16[128,1024]{1,0:T(8,128)(2,1)S(1)}, u32[]{:S(2)}, u32[]{:S(2)}) collective-permute-start(bf16[128,1024]{1,0:T(8,128)(2,1)} %collective-permute-done.refs_1_), channel_id=1, source_target_pairs={{0,2},{2,0},{4,6},{6,4},{8,10},{10,8},{12,14},{14,12},{16,18},{18,... | collective-permute-start | bytes 786440 | tf_op jit(solution)/shard_map/ppermute | solution.py:37
  58.2 56.9 %all-to-all-start.1 = ((bf16[16,32,1536]{2,1,0:T(8,128)(2,1)}), bf16[16,32,1536]{2,1,0:T(8,128)(2,1)S(1)}, u32[]{:S(2)}, u32[]{:S(2)}) async-start(bf16[16,32,1536]{2,1,0:T(8,128)(2,1)} %pad_maximum_fusion), calls=%async_computation.1 | async-start | bytes 3145728 | tf_op jit(solution)/shard_map/all_to_all | solution.py:865
  64.5 325.2 %reduce-scatter.2.cloned.1.call-start = ((), (), s32[]{:S(2)}) async-start(), calls=%async_computation.5 | async-start | bytes 6684672 | tf_op jit(solution)/shard_map/reduce_scatter | solution.py:1012
  89.0 34.8 %copy-start.16 = (bf16[64,2048]{1,0:T(8,128)(2,1)S(1)}, bf16[64,2048]{1,0:T(8,128)(2,1)}, u32[]{:S(2)}) copy-start(bf16[64,2048]{1,0:T(8,128)(2,1)} %get-tuple-element.57.refs_0_) | copy-start | bytes 786436
  89.0 19.9 %collective-permute-start.16 = (bf16[64,2048]{1,0:T(8,128)(2,1)}, bf16[64,2048]{1,0:T(8,128)(2,1)S(1)}, u32[]{:S(2)}, u32[]{:S(2)}) collective-permute-start(bf16[64,2048]{1,0:T(8,128)(2,1)} %get-tuple-element.57.refs_0_), channel_id=1, source_target_pairs={{0,8},{2,10},{4,12},{6,14},{8,16},{10,18},{12,20},{14,22},{16,24},... | collective-permute-start | bytes 786440 | tf_op jit(solution)/shard_map/ppermute | solution.py:37
  90.9 24.1 %collective-permute-start.17 = (bf16[64,2048]{1,0:T(8,128)(2,1)}, bf16[64,2048]{1,0:T(8,128)(2,1)S(1)}, u32[]{:S(2)}, u32[]{:S(2)}) collective-permute-start(bf16[64,2048]{1,0:T(8,128)(2,1)} %get-tuple-element.57.refs_0_), channel_id=1, source_target_pairs={{0,24},{2,26},{4,28},{6,30},{8,0},{10,2},{12,4},{14,6},{16,8},{18,... | collective-permute-start | bytes 786440 | tf_op jit(solution)/shard_map/ppermute | solution.py:37
  108.9 46.1 %copy-start.8 = (bf16[64,2048]{1,0:T(8,128)(2,1)}, bf16[64,2048]{1,0:T(8,128)(2,1)S(1)}, u32[]{:S(2)}) copy-start(bf16[64,2048]{1,0:T(8,128)(2,1)S(1)} %collective-permute-done.16.refs_2_) | copy-start | bytes 786436
  115.0 46.5 %copy-start.9 = (bf16[64,2048]{1,0:T(8,128)(2,1)}, bf16[64,2048]{1,0:T(8,128)(2,1)S(1)}, u32[]{:S(2)}) copy-start(bf16[64,2048]{1,0:T(8,128)(2,1)S(1)} %collective-permute-done.17.refs_6_) | copy-start | bytes 786436
  115.3 40.3 %collective-permute-start.19 = (bf16[16,32,1024]{2,1,0:T(8,128)(2,1)S(1)}, bf16[16,32,1024]{2,1,0:T(8,128)(2,1)S(1)}, u32[]{:S(2)}, u32[]{:S(2)}) collective-permute-start(bf16[16,32,1024]{2,1,0:T(8,128)(2,1)S(1)} %get-tuple-element.154), channel_id=1, source_target_pairs={{0,1},{1,0},{2,3},{3,2},{4,5},{5,4},{6,7},{7,6},{8,9},{9,8},{10,11... | collective-permute-start | bytes 3145736 | tf_op jit(solution)/shard_map/ppermute | solution.py:855
  117.4 37.6 %collective-permute-start.20 = (bf16[128,2048]{1,0:T(8,128)(2,1)S(1)}, bf16[128,2048]{1,0:T(8,128)(2,1)S(1)}, u32[]{:S(2)}, u32[]{:S(2)}) collective-permute-start(bf16[128,2048]{1,0:T(8,128)(2,1)S(1)} %pad_maximum_fusion.4), channel_id=1, source_target_pairs={{0,4},{2,6},{4,0},{6,2},{8,12},{10,14},{12,8},{14,10},{16,20},{18,... | collective-permute-start | bytes 1572872 | tf_op jit(solution)/shard_map/ppermute | solution.py:37
  123.8 30.7 %collective-permute-start.15 = (bf16[64,2048]{1,0:T(8,128)(2,1)S(1)}, bf16[64,2048]{1,0:T(8,128)(2,1)}, u32[]{:S(2)}, u32[]{:S(2)}) collective-permute-start(bf16[64,2048]{1,0:T(8,128)(2,1)S(1)} %copy-done.16), channel_id=1, source_target_pairs={{0,16},{2,18},{4,20},{6,22},{8,24},{10,26},{12,28},{14,30},{16,0},... | collective-permute-start | bytes 786440 | tf_op jit(solution)/shard_map/ppermute | solution.py:37
  130.8 24.2 %collective-permute-start.14 = (bf16[64,2048]{1,0:T(8,128)(2,1)S(1)}, bf16[64,2048]{1,0:T(8,128)(2,1)}, u32[]{:S(2)}, u32[]{:S(2)}) collective-permute-start(bf16[64,2048]{1,0:T(8,128)(2,1)S(1)} %copy-done.16), channel_id=1, source_target_pairs={{0,4},{2,6},{4,0},{6,2},{8,12},{10,14},{12,8},{14,10},{16,20},{18,... | collective-permute-start | bytes 786440 | tf_op jit(solution)/shard_map/ppermute | solution.py:37
  131.5 30.6 %collective-permute-start.28 = (bf16[16,32,512]{2,1,0:T(8,128)(2,1)S(1)}, bf16[16,32,512]{2,1,0:T(8,128)(2,1)S(1)}, u32[]{:S(2)}, u32[]{:S(2)}) collective-permute-start(bf16[16,32,512]{2,1,0:T(8,128)(2,1)S(1)} %get-tuple-element.152), channel_id=1, source_target_pairs={{0,1},{1,0},{2,3},{3,2},{4,5},{5,4},{6,7},{7,6},{8,9},{9,8},{10,11... | collective-permute-start | bytes 1572872 | tf_op jit(solution)/shard_map/ppermute | solution.py:855
  154.5 7.0 %collective-permute-start.18 = (bf16[64,2048]{1,0:T(8,128)(2,1)}, bf16[64,2048]{1,0:T(8,128)(2,1)S(1)}, u32[]{:S(2)}, u32[]{:S(2)}) collective-permute-start(bf16[64,2048]{1,0:T(8,128)(2,1)} %collective-permute-done.15.refs_4_), channel_id=1, source_target_pairs={{0,4},{2,6},{4,0},{6,2},{8,12},{10,14},{12,8},{14,10},{16,20},{18,... | collective-permute-start | bytes 786440 | tf_op jit(solution)/shard_map/ppermute | solution.py:37
  155.0 6.5 %collective-permute-start.21 = (bf16[64,2048]{1,0:T(8,128)(2,1)S(1)}, bf16[64,2048]{1,0:T(8,128)(2,1)S(1)}, u32[]{:S(2)}, u32[]{:S(2)}) collective-permute-start(bf16[64,2048]{1,0:T(8,128)(2,1)S(1)} %copy-done.16), channel_id=1, source_target_pairs={{0,2},{2,0},{4,6},{6,4},{8,10},{10,8},{12,14},{14,12},{16,18},{18,... | collective-permute-start | bytes 786440 | tf_op jit(solution)/shard_map/ppermute | solution.py:37
  155.0 7.0 %collective-permute-start.23 = (bf16[64,2048]{1,0:T(8,128)(2,1)S(1)}, bf16[64,2048]{1,0:T(8,128)(2,1)S(1)}, u32[]{:S(2)}, u32[]{:S(2)}) collective-permute-start(bf16[64,2048]{1,0:T(8,128)(2,1)S(1)} %collective-permute-done.16.refs_2_), channel_id=1, source_target_pairs={{0,2},{2,0},{4,6},{6,4},{8,10},{10,8},{12,14},{14,12},{16,18},{18,... | collective-permute-start | bytes 786440 | tf_op jit(solution)/shard_map/ppermute | solution.py:37
  155.6 8.9 %collective-permute-start.24 = (bf16[128,2048]{1,0:T(8,128)(2,1)S(1)}, bf16[128,2048]{1,0:T(8,128)(2,1)S(1)}, u32[]{:S(2)}, u32[]{:S(2)}) collective-permute-start(bf16[128,2048]{1,0:T(8,128)(2,1)S(1)} %collective-permute-done.20.refs_3_), channel_id=1, source_target_pairs={{0,2},{2,0},{4,6},{6,4},{8,10},{10,8},{12,14},{14,12},{16,18},{18,... | collective-permute-start | bytes 1572872 | tf_op jit(solution)/shard_map/ppermute | solution.py:37
  161.5 3.0 collective-permute-start.27
  161.5 3.0 collective-permute-start.25
  162.0 2.5 collective-permute-start.22
  162.8 1.8 collective-permute-start.26
  220.4 9.6 %collective-permute-start.29 = (bf16[512,2048]{1,0:T(8,128)(2,1)}, bf16[512,2048]{1,0:T(8,128)(2,1)S(1)}, u32[]{:S(2)}, u32[]{:S(2)}) collective-permute-start(bf16[512,2048]{1,0:T(8,128)(2,1)} %get-tuple-element.68), channel_id=1, source_target_pairs={{0,2},{2,0},{4,6},{6,4},{8,10},{10,8},{12,14},{14,12},{16,18},{18,... | collective-permute-start | bytes 6291464 | tf_op jit(solution)/shard_map/ppermute | solution.py:37
  223.8 39.5 %collective-permute-start.33 = (bf16[16,32,1664]{2,1,0:T(8,128)(2,1)}, bf16[16,32,1664]{2,1,0:T(8,128)(2,1)}, u32[]{:S(2)}, u32[]{:S(2)}) collective-permute-start(bf16[16,32,1664]{2,1,0:T(8,128)(2,1)} %dynamic-slice_bitcast_fusion), channel_id=1, source_target_pairs={{0,1},{1,0},{2,3},{3,2},{4,5},{5,4},{6,7},{7,6},{8,9},{9,8},{10,11... | collective-permute-start | bytes 5111816 | tf_op jit(solution)/shard_map/ppermute | solution.py:855
  231.7 19.6 %collective-permute-start.30 = (bf16[192,2048]{1,0:T(8,128)(2,1)S(1)}, bf16[192,2048]{1,0:T(8,128)(2,1)}, u32[]{:S(2)}, u32[]{:S(2)}) collective-permute-start(bf16[192,2048]{1,0:T(8,128)(2,1)S(1)} %pad_maximum_fusion.1), channel_id=1, source_target_pairs={{0,4},{2,6},{4,0},{6,2},{8,12},{10,14},{12,8},{14,10},{16,20},{18,... | collective-permute-start | bytes 2359304 | tf_op jit(solution)/shard_map/ppermute | solution.py:37
  253.3 20.2 %collective-permute-start.32 = (bf16[64,2048]{1,0:T(8,128)(2,1)S(1)}, bf16[64,2048]{1,0:T(8,128)(2,1)S(1)}, u32[]{:S(2)}, u32[]{:S(2)}) collective-permute-start(bf16[64,2048]{1,0:T(8,128)(2,1)S(1)} %get-tuple-element.142), channel_id=1, source_target_pairs={{0,16},{2,18},{4,20},{6,22},{8,24},{10,26},{12,28},{14,30},{16,0},... | collective-permute-start | bytes 786440 | tf_op jit(solution)/shard_map/ppermute | solution.py:37
  258.6 14.9 %collective-permute-start.31 = (bf16[64,2048]{1,0:T(8,128)(2,1)S(1)}, bf16[64,2048]{1,0:T(8,128)(2,1)S(1)}, u32[]{:S(2)}, u32[]{:S(2)}) collective-permute-start(bf16[64,2048]{1,0:T(8,128)(2,1)S(1)} %get-tuple-element.147), channel_id=1, source_target_pairs={{0,4},{2,6},{4,0},{6,2},{8,12},{10,14},{12,8},{14,10},{16,20},{18,... | collective-permute-start | bytes 786440 | tf_op jit(solution)/shard_map/ppermute | solution.py:37
  260.0 13.5 %collective-permute-start.34 = (bf16[64,2048]{1,0:T(8,128)(2,1)S(1)}, bf16[64,2048]{1,0:T(8,128)(2,1)S(1)}, u32[]{:S(2)}, u32[]{:S(2)}) collective-permute-start(bf16[64,2048]{1,0:T(8,128)(2,1)S(1)} %get-tuple-element.141), channel_id=1, source_target_pairs={{0,24},{2,26},{4,28},{6,30},{8,0},{10,2},{12,4},{14,6},{16,8},{18,... | collective-permute-start | bytes 786440 | tf_op jit(solution)/shard_map/ppermute | solution.py:37
  262.2 15.0 %collective-permute-start.35 = (bf16[64,2048]{1,0:T(8,128)(2,1)S(1)}, bf16[64,2048]{1,0:T(8,128)(2,1)S(1)}, u32[]{:S(2)}, u32[]{:S(2)}) collective-permute-start(bf16[64,2048]{1,0:T(8,128)(2,1)S(1)} %get-tuple-element.140), channel_id=1, source_target_pairs={{0,8},{2,10},{4,12},{6,14},{8,16},{10,18},{12,20},{14,22},{16,24},... | collective-permute-start | bytes 786440 | tf_op jit(solution)/shard_map/ppermute | solution.py:37
  304.7 18.3 %collective-permute-start.36 = (bf16[1024,1024]{1,0:T(8,128)(2,1)}, bf16[1024,1024]{1,0:T(8,128)(2,1)}, u32[]{:S(2)}, u32[]{:S(2)}) collective-permute-start(bf16[1024,1024]{1,0:T(8,128)(2,1)} %get-tuple-element.80), channel_id=1, source_target_pairs={{0,2},{2,0},{4,6},{6,4},{8,10},{10,8},{12,14},{14,12},{16,18},{18,... | collective-permute-start | bytes 6291464 | tf_op jit(solution)/shard_map/ppermute | solution.py:37
  307.9 64.8 %all-to-all-start.2 = ((bf16[16,32,1664]{2,1,0:T(8,128)(2,1)}), bf16[16,32,1664]{2,1,0:T(8,128)(2,1)S(1)}, u32[]{:S(2)}, u32[]{:S(2)}) async-start(bf16[16,32,1664]{2,1,0:T(8,128)(2,1)} %fusion), calls=%async_computation.3 | async-start | bytes 3407872 | tf_op jit(solution)/shard_map/all_to_all | solution.py:865
  325.1 30.7 %collective-permute-start.38 = (bf16[384,1024]{1,0:T(8,128)(2,1)S(1)}, bf16[384,1024]{1,0:T(8,128)(2,1)S(1)}, u32[]{:S(2)}, u32[]{:S(2)}) collective-permute-start(bf16[384,1024]{1,0:T(8,128)(2,1)S(1)} %pad_maximum_fusion.2), channel_id=1, source_target_pairs={{0,4},{2,6},{4,0},{6,2},{8,12},{10,14},{12,8},{14,10},{16,20},{18,... | collective-permute-start | bytes 2359304 | tf_op jit(solution)/shard_map/ppermute | solution.py:37
  327.1 30.5 %collective-permute-start.43 = (bf16[16,32,256]{2,1,0:T(8,128)(2,1)S(1)}, bf16[16,32,256]{2,1,0:T(8,128)(2,1)S(1)}, u32[]{:S(2)}, u32[]{:S(2)}) collective-permute-start(bf16[16,32,256]{2,1,0:T(8,128)(2,1)S(1)} %dynamic-slice_bitcast_fusion.1), channel_id=1, source_target_pairs={{0,1},{1,0},{2,3},{3,2},{4,5},{5,4},{6,7},{7,6},{8,9},{9,8},{10,11... | collective-permute-start | bytes 786440 | tf_op jit(solution)/shard_map/ppermute | solution.py:855
  357.7 1.4 collective-permute-start.44
  359.2 7.0 %collective-permute-start.45 = (bf16[4,2,32,256]{3,2,1,0:T(8,128)(2,1)S(1)}, bf16[4,2,32,256]{3,2,1,0:T(8,128)(2,1)S(1)}, u32[]{:S(2)}, u32[]{:S(2)}) collective-permute-start(bf16[4,2,32,256]{3,2,1,0:T(8,128)(2,1)S(1)} %bitcast.110), channel_id=1, source_target_pairs={{0,4},{2,6},{4,0},{6,2},{8,12},{10,14},{12,8},{14,10},{16,20},{18,... | collective-permute-start | bytes 393224 | tf_op jit(solution)/shard_map/ppermute | solution.py:37
  362.2 34.4 %collective-permute-start.37 = (bf16[128,1024]{1,0:T(8,128)(2,1)S(1)}, bf16[128,1024]{1,0:T(8,128)(2,1)S(1)}, u32[]{:S(2)}, u32[]{:S(2)}) collective-permute-start(bf16[128,1024]{1,0:T(8,128)(2,1)S(1)} %get-tuple-element.143), channel_id=1, source_target_pairs={{0,4},{2,6},{4,0},{6,2},{8,12},{10,14},{12,8},{14,10},{16,20},{18,... | collective-permute-start | bytes 786440 | tf_op jit(solution)/shard_map/ppermute | solution.py:37
  362.3 34.4 %collective-permute-start.39 = (bf16[128,1024]{1,0:T(8,128)(2,1)S(1)}, bf16[128,1024]{1,0:T(8,128)(2,1)}, u32[]{:S(2)}, u32[]{:S(2)}) collective-permute-start(bf16[128,1024]{1,0:T(8,128)(2,1)S(1)} %get-tuple-element.137), channel_id=1, source_target_pairs={{0,16},{2,18},{4,20},{6,22},{8,24},{10,26},{12,28},{14,30},{16,0},... | collective-permute-start | bytes 786440 | tf_op jit(solution)/shard_map/ppermute | solution.py:37
  366.9 26.4 %copy-start.14 = (f32[128,1024]{1,0:T(8,128)S(1)}, f32[128,1024]{1,0:T(8,128)}, u32[]{:S(2)}) copy-start(f32[128,1024]{1,0:T(8,128)} %get-tuple-element.65) | copy-start | bytes 1572868
  366.9 13.8 %collective-permute-start.46 = (bf16[4,32,256]{2,1,0:T(8,128)(2,1)}, bf16[4,32,256]{2,1,0:T(8,128)(2,1)}, u32[]{:S(2)}, u32[]{:S(2)}) collective-permute-start(bf16[4,32,256]{2,1,0:T(8,128)(2,1)} %get-tuple-element.157), channel_id=1, source_target_pairs={{0,24},{2,26},{4,28},{6,30},{8,0},{10,2},{12,4},{14,6},{16,8},{18,... | collective-permute-start | bytes 196616 | tf_op jit(solution)/shard_map/ppermute | solution.py:37
  369.8 16.1 %collective-permute-start.47 = (bf16[4,32,256]{2,1,0:T(8,128)(2,1)}, bf16[4,32,256]{2,1,0:T(8,128)(2,1)}, u32[]{:S(2)}, u32[]{:S(2)}) collective-permute-start(bf16[4,32,256]{2,1,0:T(8,128)(2,1)} %get-tuple-element.158), channel_id=1, source_target_pairs={{0,16},{2,18},{4,20},{6,22},{8,24},{10,26},{12,28},{14,30},{16,0},... | collective-permute-start | bytes 196616 | tf_op jit(solution)/shard_map/ppermute | solution.py:37
  372.7 13.2 %collective-permute-start.48 = (bf16[4,32,256]{2,1,0:T(8,128)(2,1)}, bf16[4,32,256]{2,1,0:T(8,128)(2,1)}, u32[]{:S(2)}, u32[]{:S(2)}) collective-permute-start(bf16[4,32,256]{2,1,0:T(8,128)(2,1)} %get-tuple-element.155), channel_id=1, source_target_pairs={{0,8},{2,10},{4,12},{6,14},{8,16},{10,18},{12,20},{14,22},{16,24},... | collective-permute-start | bytes 196616 | tf_op jit(solution)/shard_map/ppermute | solution.py:37
  377.9 19.8 %copy-start.4 = (bf16[1,128,1024]{2,1,0:T(8,128)(2,1)S(1)}, bf16[1,128,1024]{2,1,0:T(8,128)(2,1)}, u32[]{:S(2)}) copy-start(bf16[1,128,1024]{2,1,0:T(8,128)(2,1)} %param.17) | copy-start | bytes 786436
  380.7 16.0 %collective-permute-start.41 = (bf16[128,1024]{1,0:T(8,128)(2,1)S(1)}, bf16[128,1024]{1,0:T(8,128)(2,1)S(1)}, u32[]{:S(2)}, u32[]{:S(2)}) collective-permute-start(bf16[128,1024]{1,0:T(8,128)(2,1)S(1)} %get-tuple-element.139), channel_id=1, source_target_pairs={{0,24},{2,26},{4,28},{6,30},{8,0},{10,2},{12,4},{14,6},{16,8},{18,... | collective-permute-start | bytes 786440 | tf_op jit(solution)/shard_map/ppermute | solution.py:37
  385.9 11.7 %collective-permute-start.42 = (bf16[128,1024]{1,0:T(8,128)(2,1)S(1)}, bf16[128,1024]{1,0:T(8,128)(2,1)S(1)}, u32[]{:S(2)}, u32[]{:S(2)}) collective-permute-start(bf16[128,1024]{1,0:T(8,128)(2,1)S(1)} %get-tuple-element.138), channel_id=1, source_target_pairs={{0,8},{2,10},{4,12},{6,14},{8,16},{10,18},{12,20},{14,22},{16,24},... | collective-permute-start | bytes 786440 | tf_op jit(solution)/shard_map/ppermute | solution.py:37
  390.7 5.3 %collective-permute-start.40 = (f32[32,1024]{1,0:T(8,128)S(1)}, f32[32,1024]{1,0:T(8,128)S(1)}, u32[]{:S(2)}, u32[]{:S(2)}) collective-permute-start(f32[32,1024]{1,0:T(8,128)S(1)} %dynamic-slice_bitcast_fusion.2), channel_id=1, source_target_pairs={{0,1},{1,0},{2,3},{3,2},{4,5},{5,4},{6,7},{7,6},{8,9},{9,8},{10,11... | collective-permute-start | bytes 393224 | tf_op jit(solution)/shard_map/ppermute | solution.py:855
  (22 other events, 54.4 us)
Sparse Core Ops, SparseCore 0:
  11.1 73.7 all-gather.3
  87.2 79.3 all-gather.5
  253.4 107.4 reduce-scatter.1
where the time goes:
time: 408 us; the launch traced here: 406 us
  Pallas kernels  138 us (34%)
  waiting for transfers between devices  118 us (29%)
  starting transfers between devices  87 us (21%)
  local copies, waits for them, and re-layouts  25.2 us (6%)
  other arithmetic  23.8 us (6%)
  between operations  14.4 us (4%)
    ppermute x43, waiting for transfers between devices, permute(): return lax.ppermute(values, 'ctx', pairs)  110 us
    ppermute x43, starting transfers between devices, permute(): return lax.ppermute(values, 'ctx', pairs)  62.8 us
    pallas_call x1, Pallas kernels, expert_main(): pl.pallas_call(functools.partial(back_kernel, part, count), out_shape=(ou...  49.9 us
    pallas_call x1, Pallas kernels, head_forward(): pl.pallas_call(functools.partial(head_kernel, count // 2, band), out_shap...  18.4 us
    all_to_all x3, starting transfers between devices, exchange(): return lax.all_to_all(split, 'ctx', 0, 0, tiled=True)  17.8 us
    pallas_call x2, Pallas kernels, pull_heads(): pl.pallas_call(functools.partial(pull_kernel, last), out_shape=(jax.Shape...  16 us
    pallas_call x1, Pallas kernels, attend_backward(): pl.pallas_call(functools.partial(attend_kernel, count // 2, band), out_sh...  15.8 us
    pallas_call x1, Pallas kernels, output_weights(): pl.pallas_call(output_kernel, out_shape=jax.ShapeDtypeStruct(moe.shape, B...  10.9 us
  transfers between devices with their start and end apart: 55, of which 17 were waited for; matrix products, arithmetic and copies ran while one was open for 10% of the time, Pallas kernels for 22%

commit v1 on v0

--- a/solution.py
+++ b/solution.py
@@ -340,7 +340,7 @@
                 a_store[spot, :] = result[j * block_len : (j + 1) * block_len]
             return carry
 
-        lax.fori_loop(0, total // QUERY_BLOCK, step_fn, 0)
+        lax.fori_loop(0, total // QUERY_BLOCK, step_fn, 0, unroll=total // QUERY_BLOCK <= 8)
         for j in range(total // QUERY_BLOCK):
             part = a_store[j * QUERY_BLOCK : (j + 1) * QUERY_BLOCK, :]
             att_ref[:, j * QUERY_BLOCK : (j + 1) * QUERY_BLOCK] = part.T[:HD].astype(BF)
@@ -637,7 +637,7 @@
             own_ref[pl.ds(first, block_len), :] = jnp.where(keep, piece, jnp.zeros_like(piece))
         return carry
 
-    lax.fori_loop(0, total // QUERY_BLOCK, turn, 0)
+    lax.fori_loop(0, total // QUERY_BLOCK, turn, 0, unroll=total // QUERY_BLOCK <= 8)
 
 
 def attend_backward(heads_all, upstream, logs, tables, ids, spots, firsts, where, count, band):

time: 408 us -> 408 us (level)
  transfers between devices with their start and end apart: 55 -> 55, of which waited for: 17 -> 17; matrix products, arithmetic and copies ran while one was open for 10% -> 10% of each run, Pallas kernels for 22% -> 21%
where the time goes in v1:
time: 408 us; the launch traced here: 406 us
  Pallas kernels  135 us (33%)
  waiting for transfers between devices  118 us (29%)
  starting transfers between devices  89.4 us (22%)
  local copies, waits for them, and re-layouts  25.2 us (6%)
  other arithmetic  23.8 us (6%)
  between operations  14.4 us (4%)
    ppermute x43, waiting for transfers between devices, permute(): return lax.ppermute(values, 'ctx', pairs)  110 us
    ppermute x43, starting transfers between devices, permute(): return lax.ppermute(values, 'ctx', pairs)  65.5 us
    pallas_call x1, Pallas kernels, expert_main(): pl.pallas_call(functools.partial(back_kernel, part, count), out_shape=(ou...  49.9 us
    all_to_all x3, starting transfers between devices, exchange(): return lax.all_to_all(split, 'ctx', 0, 0, tiled=True)  17.4 us
    pallas_call x1, Pallas kernels, head_forward(): pl.pallas_call(functools.partial(head_kernel, count // 2, band), out_shap...  16.6 us
    pallas_call x2, Pallas kernels, pull_heads(): pl.pallas_call(functools.partial(pull_kernel, last), out_shape=(jax.Shape...  16 us
    pallas_call x1, Pallas kernels, attend_backward(): pl.pallas_call(functools.partial(attend_kernel, count // 2, band), out_sh...  15.2 us
    pallas_call x1, Pallas kernels, output_weights(): pl.pallas_call(output_kernel, out_shape=jax.ShapeDtypeStruct(moe.shape, B...  10.9 us
  transfers between devices with their start and end apart: 55, of which 17 were waited for; matrix products, arithmetic and copies ran while one was open for 10% of the time, Pallas kernels for 21%

profile of v1, /device:TPU:0, one launch (start us, length us, event | category | flops | bytes accessed | tf_op | source)
XLA Modules:
  0.0 406.2 jit_solution(15111403809092959077)
XLA Ops:
  8.8 1.8 concatenate.27
  10.6 3.1 collective-permute-start.4
  13.7 2.1 collective-permute-start.5
  18.5 1.7 pack_small.1
  20.3 4.3 %all-to-all-start = ((bf16[16,32,256]{2,1,0:T(8,128)(2,1)}), bf16[16,32,256]{2,1,0:T(8,128)(2,1)S(1)}, u32[]{:S(2)}, u32[]{:S(2)}) async-start(bf16[16,32,256]{2,1,0:T(8,128)(2,1)} %pack_small.1), calls=%async_computation | async-start | bytes 524288 | tf_op jit(solution)/shard_map/all_to_all | solution.py:865
  24.5 3.2 collective-permute-done.5.refs_6_
  27.8 1.6 collective-permute-start.6
  30.5 5.3 %all-to-all-done = bf16[16,32,256]{2,1,0:T(8,128)(2,1)S(1)} async-done(((bf16[16,32,256]{2,1,0:T(8,128)(2,1)}), bf16[16,32,256]{2,1,0:T(8,128)(2,1)S(1)}, u32[]{:S(2)}, u32[]{:S(2)}) %all-to-all-start) | async-done | bytes 262176 | tf_op jit(solution)/shard_map/all_to_all | solution.py:865
  35.8 1.5 collective-permute-start.3
  37.3 5.7 %collective-permute-start.7 = (bf16[128,1024]{1,0:T(8,128)(2,1)}, bf16[128,1024]{1,0:T(8,128)(2,1)}, u32[]{:S(2)}, u32[]{:S(2)}) collective-permute-start(bf16[128,1024]{1,0:T(8,128)(2,1)} %bitcast.3.refs_0_), channel_id=1, source_target_pairs={{0,2},{2,0},{4,6},{6,4},{8,10},{10,8},{12,14},{14,12},{16,18},{18,... | collective-permute-start | bytes 786440 | tf_op jit(solution)/shard_map/ppermute | solution.py:37
  43.6 2.8 collective-permute-done.1.refs_4_
  46.4 1.5 collective-permute-start.2
  53.3 2.4 split_weights.1
  58.2 6.4 %all-to-all-start.1 = ((bf16[16,32,1536]{2,1,0:T(8,128)(2,1)}), bf16[16,32,1536]{2,1,0:T(8,128)(2,1)S(1)}, u32[]{:S(2)}, u32[]{:S(2)}) async-start(bf16[16,32,1536]{2,1,0:T(8,128)(2,1)} %pad_maximum_fusion), calls=%async_computation.1 | async-start | bytes 3145728 | tf_op jit(solution)/shard_map/all_to_all | solution.py:865
  65.6 5.0 %join_hidden.1 = bf16[16,128,1024]{2,1,0:T(8,128)(2,1)} custom-call(s32[16]{0:T(128)} %fusion.13.places.heads.every, bf16[128,1024]{1,0:T(8,128)(2,1)} %bitcast.3.refs_0_, bf16[128,1024]{1,0:T(8,128)(2,1)} %collective-permute-done.refs_1_, bf16[128,1024]{1,0:T(8,128)(2,1)} %copy-done.6, bf16[256,1024]{1,0:T(8,128)(2,1)} %copy-done.10, ...), custom_call_target="tpu_custom_call" | custom-call | flops 20 | bytes 167772160 | tf_op jit(solution)/shard_map/join_hidden/pallas_call | solution.py:151
  70.5 16.6 %head_forward.1 = (bf16[2048,512]{1,0:T(8,128)(2,1)}, f32[2048,1]{1,0:T(8,128)}, bf16[64,2048]{1,0:T(8,128)(2,1)}) custom-call(s32[32]{0:T(128)} %bitcast.120, s32[32]{0:T(128)} %select_reduce_fusion.spots, s32[16]{0:T(128)} %select_reduce_fusion.1.firsts, bf16[2048,1024]{1,0:T(8,128)(2,1)} %bitcast.82, bf16[1024,384]{1,0:T(8,128)(2,1)} %get-tuple-element.53.w_ref, ...), custom_call_target="tpu_custom_call" | custom-call | flops 32212254720 | bytes 83886080 | tf_op jit(solution)/shard_map/head_forward/pallas_call | solution.py:352
  87.2 2.0 collective-permute-start.16
  89.1 2.1 collective-permute-start.17
  91.2 17.7 %collective-permute-done.16.refs_2_ = bf16[64,2048]{1,0:T(8,128)(2,1)S(1)} collective-permute-done((bf16[64,2048]{1,0:T(8,128)(2,1)}, bf16[64,2048]{1,0:T(8,128)(2,1)S(1)}, u32[]{:S(2)}, u32[]{:S(2)}) %collective-permute-start.16) | collective-permute-done | bytes 262176 | tf_op jit(solution)/shard_map/ppermute | solution.py:37
  108.9 3.3 collective-permute-done.17.refs_6_
  112.5 1.8 collective-permute-start.19
  114.4 5.8 %collective-permute-start.20 = (bf16[128,2048]{1,0:T(8,128)(2,1)S(1)}, bf16[128,2048]{1,0:T(8,128)(2,1)S(1)}, u32[]{:S(2)}, u32[]{:S(2)}) collective-permute-start(bf16[128,2048]{1,0:T(8,128)(2,1)S(1)} %pad_maximum_fusion.4), channel_id=1, source_target_pairs={{0,4},{2,6},{4,0},{6,2},{8,12},{10,14},{12,8},{14,10},{16,20},{18,... | collective-permute-start | bytes 1572872 | tf_op jit(solution)/shard_map/ppermute | solution.py:37
  120.2 10.7 %collective-permute-start.15 = (bf16[64,2048]{1,0:T(8,128)(2,1)S(1)}, bf16[64,2048]{1,0:T(8,128)(2,1)}, u32[]{:S(2)}, u32[]{:S(2)}) collective-permute-start(bf16[64,2048]{1,0:T(8,128)(2,1)S(1)} %copy-done.16), channel_id=1, source_target_pairs={{0,16},{2,18},{4,20},{6,22},{8,24},{10,26},{12,28},{14,30},{16,0},... | collective-permute-start | bytes 786440 | tf_op jit(solution)/shard_map/ppermute | solution.py:37
  132.0 22.1 %collective-permute-done.15.refs_4_ = bf16[64,2048]{1,0:T(8,128)(2,1)} collective-permute-done((bf16[64,2048]{1,0:T(8,128)(2,1)S(1)}, bf16[64,2048]{1,0:T(8,128)(2,1)}, u32[]{:S(2)}, u32[]{:S(2)}) %collective-permute-start.15) | collective-permute-done | bytes 262176 | tf_op jit(solution)/shard_map/ppermute | solution.py:37
  156.3 1.6 copy.67
  157.9 3.4 collective-permute-done.18.refs_5_
  165.4 4.9 %join_heads.1.att_ref = bf16[16,64,2048]{2,1,0:T(8,128)(2,1)} custom-call(s32[16]{0:T(128)} %fusion.13.places.heads.every, bf16[64,2048]{1,0:T(8,128)(2,1)} %get-tuple-element.57.refs_0_, bf16[64,2048]{1,0:T(8,128)(2,1)} %collective-permute-done.14.refs_1_, bf16[64,2048]{1,0:T(8,128)(2,1)} %copy-done.8, bf16[128,2048]{1,0:T(8,128)(2,1)} %copy-done.11, ...), custom_call_target="tpu_custom_call" | custom-call | flops 20 | bytes 167772160 | tf_op jit(solution)/shard_map/join_heads/pallas_call | solution.py:151
  170.3 49.9 %expert_main.1 = (bf16[2048,512]{1,0:T(8,128)(2,1)}, bf16[2048,1024]{1,0:T(8,128)(2,1)}, bf16[512,2048]{1,0:T(8,128)(2,1)}, bf16[512,2048]{1,0:T(8,128)(2,1)}, b...) custom-call(s32[16]{0:T(128)} %fusion.13.places.heads.every, s32[4]{0:T(128)} %pad_add_fusion.where, ...), custom_call_target="tpu_custom_call" | custom-call | flops 51539607552 | bytes 50331648 | tf_op jit(solution)/shard_map/expert_main/pallas_call | solution.py:490
  220.8 2.8 dynamic-slice_bitcast_fusion
  223.9 6.3 %moe_out.1.moe_ref = bf16[16,192,1024]{2,1,0:T(8,128)(2,1)} custom-call(bf16[2048,512]{1,0:T(8,128)(2,1)} %get-tuple-element.70.act_ref, bf16[1024,512]{1,0:T(8,128)(2,1)} %bitcast.97), custom_call_target="tpu_custom_call" | custom-call | flops 42949672960 | bytes 125829120 | tf_op jit(solution)/shard_map/moe_out/pallas_call | solution.py:533
  231.8 1.4 collective-permute-start.30
  233.2 10.9 %output_weights.1 = bf16[16,192,1024]{2,1,0:T(8,128)(2,1)} custom-call(s32[4]{0:T(128)} %pad_add_fusion.where, bf16[16,64,2048]{2,1,0:T(8,128)(2,1)} %join_heads.1.att_ref, bf16[2048,1024]{1,0:T(8,128)(2,1)} %get-tuple-element.69.v_ref.gm_ref.hm_ref, bf16[16,128,1152]{2,1,0:T(8,128)(2,1)} %bitcast.115, ...), custom_call_target="tpu_custom_call", output_to_operand_aliasing={{}: (4, {})} | custom-call | flops 85899345920 | bytes 335544320 | tf_op jit(solution)/shard_map/output_weights/pallas_call | solution.py:569
  244.1 7.1 %collective-permute-done.30 = bf16[192,2048]{1,0:T(8,128)(2,1)} collective-permute-done((bf16[192,2048]{1,0:T(8,128)(2,1)S(1)}, bf16[192,2048]{1,0:T(8,128)(2,1)}, u32[]{:S(2)}, u32[]{:S(2)}) %collective-permute-start.30) | collective-permute-done | bytes 786464 | tf_op jit(solution)/shard_map/ppermute | solution.py:37
  251.2 1.9 add_convert_fusion.8
  253.1 5.4 %collective-permute-start.32 = (bf16[64,2048]{1,0:T(8,128)(2,1)S(1)}, bf16[64,2048]{1,0:T(8,128)(2,1)S(1)}, u32[]{:S(2)}, u32[]{:S(2)}) collective-permute-start(bf16[64,2048]{1,0:T(8,128)(2,1)S(1)} %get-tuple-element.142), channel_id=1, source_target_pairs={{0,16},{2,18},{4,20},{6,22},{8,24},{10,26},{12,28},{14,30},{16,0},... | collective-permute-start | bytes 786440 | tf_op jit(solution)/shard_map/ppermute | solution.py:37
  258.6 1.5 collective-permute-start.31
  260.0 1.6 collective-permute-start.34
  263.0 10.5 %collective-permute-done.32 = bf16[64,2048]{1,0:T(8,128)(2,1)S(1)} collective-permute-done((bf16[64,2048]{1,0:T(8,128)(2,1)S(1)}, bf16[64,2048]{1,0:T(8,128)(2,1)S(1)}, u32[]{:S(2)}, u32[]{:S(2)}) %collective-permute-start.32) | collective-permute-done | bytes 262176 | tf_op jit(solution)/shard_map/ppermute | solution.py:37
  273.5 3.7 collective-permute-done.35
  277.2 2.0 convert_add_fusion.2.up_ref
  279.1 15.2 %attend_backward.1.g_ref.h_ref = bf16[2048,256]{1,0:T(8,128)(2,1)} custom-call(s32[32]{0:T(128)} %bitcast.121, s32[32]{0:T(128)} %select_reduce_fusion.spots, s32[16]{0:T(128)} %select_reduce_fusion.1.firsts, s32[4]{0:T(128)} %pad_add_fusion.where, bf16[2048,512]{1,0:T(8,128)(2,1)} %get-tuple-element.72.all_ref, f32[64,2048]{1,0:T(8,128)} %convert_add_fusion.2.up_ref, ...), custom_call_target="tpu_custom_call" | custom-call | flops 40265318400 | bytes 83886080 | tf_op jit(solution)/shard_map/attend_backward/pallas_call | solution.py:646
  296.0 8.1 %pull_first.1 = (bf16[1024,1024]{1,0:T(8,128)(2,1)}, f32[1024,256]{1,0:T(8,128)}, f32[8,1024]{1,0:T(8,128)}) custom-call(s32[8]{0:T(128)} %get-tuple-element.164.order, s32[16]{0:T(128)} %fusion.13.places.heads.every, bf16[2048,256]{1,0:T(8,128)(2,1)} %attend_backward.1.g_ref.h_ref, bf16[2048,256]{1,0:T(8,128)(2,1)} %attend_backward.1.g_ref.h_ref, ...), custom_call_target="tpu_custom_call" | custom-call | flops 1073741824 | bytes 6291456 | tf_op jit(solution)/shard_map/pull_first/pallas_call | solution.py:718
  304.2 3.1 fusion
  307.4 6.8 %all-to-all-start.2 = ((bf16[16,32,1664]{2,1,0:T(8,128)(2,1)}), bf16[16,32,1664]{2,1,0:T(8,128)(2,1)S(1)}, u32[]{:S(2)}, u32[]{:S(2)}) async-start(bf16[16,32,1664]{2,1,0:T(8,128)(2,1)} %fusion), calls=%async_computation.3 | async-start | bytes 3407872 | tf_op jit(solution)/shard_map/all_to_all | solution.py:865
  314.1 7.9 %pull_last.1 = (bf16[1024,1024]{1,0:T(8,128)(2,1)}, bf16[1024,256]{1,0:T(8,128)(2,1)}, f32[8,1024]{1,0:T(8,128)}) custom-call(s32[8]{0:T(128)} %get-tuple-element.163.order, s32[16]{0:T(128)} %fusion.13.places.heads.every, bf16[2048,256]{1,0:T(8,128)(2,1)} %attend_backward.1.g_ref.h_ref, bf16[2048,256]{1,0:T(8,128)(2,1)} %attend_backward.1.g_ref.h_ref, ...), custom_call_target="tpu_custom_call" | custom-call | flops 1073741824 | bytes 6291456 | tf_op jit(solution)/shard_map/pull_last/pallas_call | solution.py:718
  322.1 1.9 add_convert_fusion.6
  324.1 1.9 collective-permute-start.38
  326.8 29.7 %collective-permute-done.38 = bf16[384,1024]{1,0:T(8,128)(2,1)S(1)} collective-permute-done((bf16[384,1024]{1,0:T(8,128)(2,1)S(1)}, bf16[384,1024]{1,0:T(8,128)(2,1)S(1)}, u32[]{:S(2)}, u32[]{:S(2)}) %collective-permute-start.38) | collective-permute-done | bytes 786464 | tf_op jit(solution)/shard_map/ppermute | solution.py:37
  356.4 1.8 add_convert_fusion.2
  359.8 1.4 collective-permute-start.45
  362.4 1.4 collective-permute-start.39
  363.8 2.4 collective-permute-done.45
  366.9 1.9 collective-permute-start.46
  368.9 3.2 collective-permute-start.47
  373.3 3.9 finish_experts.1
  377.2 1.4 copy.73
  378.7 1.4 slice_reduce_fusion
  380.1 3.8 collective-permute-start.41
  383.9 1.5 collective-permute-done.47.refs_2_
  385.4 2.4 finish_heads.1
  387.8 1.4 slice_reduce_fusion.1
  390.2 1.6 collective-permute-start.40
  393.7 1.9 collective-permute-done.40
  397.4 2.2 add_bitcast_fusion
  (180 shorter events, 38.3 us)
Async XLA Ops:
  7.2 35.8 %copy-start.29 = (s32[1,16]{1,0:T(1,128)S(1)}, s32[1,16]{1,0:T(1,128)}, u32[]{:S(2)}) copy-start(s32[1,16]{1,0:T(1,128)} %param.18) | copy-start | bytes 196
  7.2 41.5 %copy-start.5 = (bf16[32,16384]{1,0:T(8,128)(2,1)S(1)}, bf16[32,16384]{1,0:T(8,128)(2,1)}, u32[]{:S(2)}) copy-start(bf16[32,16384]{1,0:T(8,128)(2,1)} %param.28) | copy-start | bytes 3145732
  7.2 163.1 %all-gather.4.cloned.1.call-start = ((), (), s32[]{:S(2)}) async-start(), calls=%async_computation.4 | async-start | bytes 2162688 | tf_op jit(solution)/shard_map/all_gather | solution.py:904
  7.9 162.4 %all-gather.6.cloned.1.call-start = ((), (), s32[]{:S(2)}) async-start(), calls=%async_computation.6 | async-start | bytes 5013504 | tf_op jit(solution)/shard_map/all_gather | solution.py:905
  10.6 13.9 %collective-permute-start.4 = (bf16[128,1024]{1,0:T(8,128)(2,1)}, bf16[128,1024]{1,0:T(8,128)(2,1)S(1)}, u32[]{:S(2)}, u32[]{:S(2)}) collective-permute-start(bf16[128,1024]{1,0:T(8,128)(2,1)} %bitcast.3.refs_0_), channel_id=1, source_target_pairs={{0,8},{2,10},{4,12},{6,14},{8,16},{10,18},{12,20},{14,22},{16,24},... | collective-permute-start | bytes 786440 | tf_op jit(solution)/shard_map/ppermute | solution.py:37
  13.7 14.1 %collective-permute-start.5 = (bf16[128,1024]{1,0:T(8,128)(2,1)}, bf16[128,1024]{1,0:T(8,128)(2,1)S(1)}, u32[]{:S(2)}, u32[]{:S(2)}) collective-permute-start(bf16[128,1024]{1,0:T(8,128)(2,1)} %bitcast.3.refs_0_), channel_id=1, source_target_pairs={{0,24},{2,26},{4,28},{6,30},{8,0},{10,2},{12,4},{14,6},{16,8},{18,... | collective-permute-start | bytes 786440 | tf_op jit(solution)/shard_map/ppermute | solution.py:37
  20.3 15.6 %all-to-all-start = ((bf16[16,32,256]{2,1,0:T(8,128)(2,1)}), bf16[16,32,256]{2,1,0:T(8,128)(2,1)S(1)}, u32[]{:S(2)}, u32[]{:S(2)}) async-start(bf16[16,32,256]{2,1,0:T(8,128)(2,1)} %pack_small.1), calls=%async_computation | async-start | bytes 524288 | tf_op jit(solution)/shard_map/all_to_all | solution.py:865
  24.5 31.2 %copy-start.6 = (bf16[128,1024]{1,0:T(8,128)(2,1)}, bf16[128,1024]{1,0:T(8,128)(2,1)S(1)}, u32[]{:S(2)}) copy-start(bf16[128,1024]{1,0:T(8,128)(2,1)S(1)} %collective-permute-done.4.refs_2_) | copy-start | bytes 786436
  27.8 22.5 %copy-start.7 = (bf16[128,1024]{1,0:T(8,128)(2,1)}, bf16[128,1024]{1,0:T(8,128)(2,1)S(1)}, u32[]{:S(2)}) copy-start(bf16[128,1024]{1,0:T(8,128)(2,1)S(1)} %collective-permute-done.5.refs_6_) | copy-start | bytes 786436
  27.8 20.2 %collective-permute-start.6 = (bf16[256,1024]{1,0:T(8,128)(2,1)S(1)}, bf16[256,1024]{1,0:T(8,128)(2,1)S(1)}, u32[]{:S(2)}, u32[]{:S(2)}) collective-permute-start(bf16[256,1024]{1,0:T(8,128)(2,1)S(1)} %pad_maximum_fusion.3), channel_id=1, source_target_pairs={{0,4},{2,6},{4,0},{6,2},{8,12},{10,14},{12,8},{14,10},{16,20},{18,... | collective-permute-start | bytes 1572872 | tf_op jit(solution)/shard_map/ppermute | solution.py:37
  29.4 17.1 %collective-permute-start.1 = (bf16[128,1024]{1,0:T(8,128)(2,1)}, bf16[128,1024]{1,0:T(8,128)(2,1)}, u32[]{:S(2)}, u32[]{:S(2)}) collective-permute-start(bf16[128,1024]{1,0:T(8,128)(2,1)} %bitcast.3.refs_0_), channel_id=1, source_target_pairs={{0,16},{2,18},{4,20},{6,22},{8,24},{10,26},{12,28},{14,30},{16,0},... | collective-permute-start | bytes 786440 | tf_op jit(solution)/shard_map/ppermute | solution.py:37
  35.8 10.6 %collective-permute-start.3 = (bf16[16,32,256]{2,1,0:T(8,128)(2,1)S(1)}, bf16[16,32,256]{2,1,0:T(8,128)(2,1)S(1)}, u32[]{:S(2)}, u32[]{:S(2)}) collective-permute-start(bf16[16,32,256]{2,1,0:T(8,128)(2,1)S(1)} %all-to-all-done), channel_id=1, source_target_pairs={{0,1},{1,0},{2,3},{3,2},{4,5},{5,4},{6,7},{7,6},{8,9},{9,8},{10,11... | collective-permute-start | bytes 786440 | tf_op jit(solution)/shard_map/ppermute | solution.py:855
  37.3 18.5 %collective-permute-start = (bf16[128,1024]{1,0:T(8,128)(2,1)}, bf16[128,1024]{1,0:T(8,128)(2,1)}, u32[]{:S(2)}, u32[]{:S(2)}) collective-permute-start(bf16[128,1024]{1,0:T(8,128)(2,1)} %bitcast.3.refs_0_), channel_id=1, source_target_pairs={{0,4},{2,6},{4,0},{6,2},{8,12},{10,14},{12,8},{14,10},{16,20},{18,... | collective-permute-start | bytes 786440 | tf_op jit(solution)/shard_map/ppermute | solution.py:37
  37.3 19.1 %collective-permute-start.7 = (bf16[128,1024]{1,0:T(8,128)(2,1)}, bf16[128,1024]{1,0:T(8,128)(2,1)}, u32[]{:S(2)}, u32[]{:S(2)}) collective-permute-start(bf16[128,1024]{1,0:T(8,128)(2,1)} %bitcast.3.refs_0_), channel_id=1, source_target_pairs={{0,2},{2,0},{4,6},{6,4},{8,10},{10,8},{12,14},{14,12},{16,18},{18,... | collective-permute-start | bytes 786440 | tf_op jit(solution)/shard_map/ppermute | solution.py:37
  46.4 10.3 %collective-permute-start.13 = (bf16[128,1024]{1,0:T(8,128)(2,1)S(1)}, bf16[128,1024]{1,0:T(8,128)(2,1)}, u32[]{:S(2)}, u32[]{:S(2)}) collective-permute-start(bf16[128,1024]{1,0:T(8,128)(2,1)S(1)} %collective-permute-done.5.refs_6_), channel_id=1, source_target_pairs={{0,2},{2,0},{4,6},{6,4},{8,10},{10,8},{12,14},{14,12},{16,18},{18,... | collective-permute-start | bytes 786440 | tf_op jit(solution)/shard_map/ppermute | solution.py:37
  46.4 9.7 %collective-permute-start.2 = (bf16[128,1024]{1,0:T(8,128)(2,1)}, bf16[128,1024]{1,0:T(8,128)(2,1)}, u32[]{:S(2)}, u32[]{:S(2)}) collective-permute-start(bf16[128,1024]{1,0:T(8,128)(2,1)} %collective-permute-done.1.refs_4_), channel_id=1, source_target_pairs={{0,4},{2,6},{4,0},{6,2},{8,12},{10,14},{12,8},{14,10},{16,20},{18,... | collective-permute-start | bytes 786440 | tf_op jit(solution)/shard_map/ppermute | solution.py:37
  48.0 16.7 %collective-permute-start.10 = (bf16[256,1024]{1,0:T(8,128)(2,1)S(1)}, bf16[256,1024]{1,0:T(8,128)(2,1)}, u32[]{:S(2)}, u32[]{:S(2)}) collective-permute-start(bf16[256,1024]{1,0:T(8,128)(2,1)S(1)} %collective-permute-done.6.refs_3_), channel_id=1, source_target_pairs={{0,2},{2,0},{4,6},{6,4},{8,10},{10,8},{12,14},{14,12},{16,18},{18,... | collective-permute-start | bytes 1572872 | tf_op jit(solution)/shard_map/ppermute | solution.py:37
  55.8 8.8 %collective-permute-start.9 = (bf16[128,1024]{1,0:T(8,128)(2,1)S(1)}, bf16[128,1024]{1,0:T(8,128)(2,1)S(1)}, u32[]{:S(2)}, u32[]{:S(2)}) collective-permute-start(bf16[128,1024]{1,0:T(8,128)(2,1)S(1)} %collective-permute-done.4.refs_2_), channel_id=1, source_target_pairs={{0,2},{2,0},{4,6},{6,4},{8,10},{10,8},{12,14},{14,12},{16,18},{18,... | collective-permute-start | bytes 786440 | tf_op jit(solution)/shard_map/ppermute | solution.py:37
  56.2 8.4 %collective-permute-start.11 = (bf16[128,1024]{1,0:T(8,128)(2,1)}, bf16[128,1024]{1,0:T(8,128)(2,1)S(1)}, u32[]{:S(2)}, u32[]{:S(2)}) collective-permute-start(bf16[128,1024]{1,0:T(8,128)(2,1)} %collective-permute-done.1.refs_4_), channel_id=1, source_target_pairs={{0,2},{2,0},{4,6},{6,4},{8,10},{10,8},{12,14},{14,12},{16,18},{18,... | collective-permute-start | bytes 786440 | tf_op jit(solution)/shard_map/ppermute | solution.py:37
  56.4 8.3 %collective-permute-start.12 = (bf16[128,1024]{1,0:T(8,128)(2,1)}, bf16[128,1024]{1,0:T(8,128)(2,1)S(1)}, u32[]{:S(2)}, u32[]{:S(2)}) collective-permute-start(bf16[128,1024]{1,0:T(8,128)(2,1)} %collective-permute-done.2.refs_5_), channel_id=1, source_target_pairs={{0,2},{2,0},{4,6},{6,4},{8,10},{10,8},{12,14},{14,12},{16,18},{18,... | collective-permute-start | bytes 786440 | tf_op jit(solution)/shard_map/ppermute | solution.py:37
  56.7 8.0 %collective-permute-start.8 = (bf16[128,1024]{1,0:T(8,128)(2,1)}, bf16[128,1024]{1,0:T(8,128)(2,1)S(1)}, u32[]{:S(2)}, u32[]{:S(2)}) collective-permute-start(bf16[128,1024]{1,0:T(8,128)(2,1)} %collective-permute-done.refs_1_), channel_id=1, source_target_pairs={{0,2},{2,0},{4,6},{6,4},{8,10},{10,8},{12,14},{14,12},{16,18},{18,... | collective-permute-start | bytes 786440 | tf_op jit(solution)/shard_map/ppermute | solution.py:37
  58.2 54.1 %all-to-all-start.1 = ((bf16[16,32,1536]{2,1,0:T(8,128)(2,1)}), bf16[16,32,1536]{2,1,0:T(8,128)(2,1)S(1)}, u32[]{:S(2)}, u32[]{:S(2)}) async-start(bf16[16,32,1536]{2,1,0:T(8,128)(2,1)} %pad_maximum_fusion), calls=%async_computation.1 | async-start | bytes 3145728 | tf_op jit(solution)/shard_map/all_to_all | solution.py:865
  64.5 324.7 %reduce-scatter.2.cloned.1.call-start = ((), (), s32[]{:S(2)}) async-start(), calls=%async_computation.5 | async-start | bytes 6684672 | tf_op jit(solution)/shard_map/reduce_scatter | solution.py:1012
  87.2 33.0 %copy-start.16 = (bf16[64,2048]{1,0:T(8,128)(2,1)S(1)}, bf16[64,2048]{1,0:T(8,128)(2,1)}, u32[]{:S(2)}) copy-start(bf16[64,2048]{1,0:T(8,128)(2,1)} %get-tuple-element.57.refs_0_) | copy-start | bytes 786436
  87.2 21.7 %collective-permute-start.16 = (bf16[64,2048]{1,0:T(8,128)(2,1)}, bf16[64,2048]{1,0:T(8,128)(2,1)S(1)}, u32[]{:S(2)}, u32[]{:S(2)}) collective-permute-start(bf16[64,2048]{1,0:T(8,128)(2,1)} %get-tuple-element.57.refs_0_), channel_id=1, source_target_pairs={{0,8},{2,10},{4,12},{6,14},{8,16},{10,18},{12,20},{14,22},{16,24},... | collective-permute-start | bytes 786440 | tf_op jit(solution)/shard_map/ppermute | solution.py:37
  89.1 23.1 %collective-permute-start.17 = (bf16[64,2048]{1,0:T(8,128)(2,1)}, bf16[64,2048]{1,0:T(8,128)(2,1)S(1)}, u32[]{:S(2)}, u32[]{:S(2)}) collective-permute-start(bf16[64,2048]{1,0:T(8,128)(2,1)} %get-tuple-element.57.refs_0_), channel_id=1, source_target_pairs={{0,24},{2,26},{4,28},{6,30},{8,0},{10,2},{12,4},{14,6},{16,8},{18,... | collective-permute-start | bytes 786440 | tf_op jit(solution)/shard_map/ppermute | solution.py:37
  108.9 46.4 %copy-start.8 = (bf16[64,2048]{1,0:T(8,128)(2,1)}, bf16[64,2048]{1,0:T(8,128)(2,1)S(1)}, u32[]{:S(2)}) copy-start(bf16[64,2048]{1,0:T(8,128)(2,1)S(1)} %collective-permute-done.16.refs_2_) | copy-start | bytes 786436
  112.2 49.1 %copy-start.9 = (bf16[64,2048]{1,0:T(8,128)(2,1)}, bf16[64,2048]{1,0:T(8,128)(2,1)S(1)}, u32[]{:S(2)}) copy-start(bf16[64,2048]{1,0:T(8,128)(2,1)S(1)} %collective-permute-done.17.refs_6_) | copy-start | bytes 786436
  112.5 43.4 %collective-permute-start.19 = (bf16[16,32,1024]{2,1,0:T(8,128)(2,1)S(1)}, bf16[16,32,1024]{2,1,0:T(8,128)(2,1)S(1)}, u32[]{:S(2)}, u32[]{:S(2)}) collective-permute-start(bf16[16,32,1024]{2,1,0:T(8,128)(2,1)S(1)} %get-tuple-element.154), channel_id=1, source_target_pairs={{0,1},{1,0},{2,3},{3,2},{4,5},{5,4},{6,7},{7,6},{8,9},{9,8},{10,11... | collective-permute-start | bytes 3145736 | tf_op jit(solution)/shard_map/ppermute | solution.py:855
  114.4 41.0 %collective-permute-start.20 = (bf16[128,2048]{1,0:T(8,128)(2,1)S(1)}, bf16[128,2048]{1,0:T(8,128)(2,1)S(1)}, u32[]{:S(2)}, u32[]{:S(2)}) collective-permute-start(bf16[128,2048]{1,0:T(8,128)(2,1)S(1)} %pad_maximum_fusion.4), channel_id=1, source_target_pairs={{0,4},{2,6},{4,0},{6,2},{8,12},{10,14},{12,8},{14,10},{16,20},{18,... | collective-permute-start | bytes 1572872 | tf_op jit(solution)/shard_map/ppermute | solution.py:37
  120.2 33.9 %collective-permute-start.15 = (bf16[64,2048]{1,0:T(8,128)(2,1)S(1)}, bf16[64,2048]{1,0:T(8,128)(2,1)}, u32[]{:S(2)}, u32[]{:S(2)}) collective-permute-start(bf16[64,2048]{1,0:T(8,128)(2,1)S(1)} %copy-done.16), channel_id=1, source_target_pairs={{0,16},{2,18},{4,20},{6,22},{8,24},{10,26},{12,28},{14,30},{16,0},... | collective-permute-start | bytes 786440 | tf_op jit(solution)/shard_map/ppermute | solution.py:37
  130.9 24.5 %collective-permute-start.14 = (bf16[64,2048]{1,0:T(8,128)(2,1)S(1)}, bf16[64,2048]{1,0:T(8,128)(2,1)}, u32[]{:S(2)}, u32[]{:S(2)}) collective-permute-start(bf16[64,2048]{1,0:T(8,128)(2,1)S(1)} %copy-done.16), channel_id=1, source_target_pairs={{0,4},{2,6},{4,0},{6,2},{8,12},{10,14},{12,8},{14,10},{16,20},{18,... | collective-permute-start | bytes 786440 | tf_op jit(solution)/shard_map/ppermute | solution.py:37
  131.5 30.4 %collective-permute-start.28 = (bf16[16,32,512]{2,1,0:T(8,128)(2,1)S(1)}, bf16[16,32,512]{2,1,0:T(8,128)(2,1)S(1)}, u32[]{:S(2)}, u32[]{:S(2)}) collective-permute-start(bf16[16,32,512]{2,1,0:T(8,128)(2,1)S(1)} %get-tuple-element.152), channel_id=1, source_target_pairs={{0,1},{1,0},{2,3},{3,2},{4,5},{5,4},{6,7},{7,6},{8,9},{9,8},{10,11... | collective-permute-start | bytes 1572872 | tf_op jit(solution)/shard_map/ppermute | solution.py:855
  154.1 7.2 %collective-permute-start.18 = (bf16[64,2048]{1,0:T(8,128)(2,1)}, bf16[64,2048]{1,0:T(8,128)(2,1)S(1)}, u32[]{:S(2)}, u32[]{:S(2)}) collective-permute-start(bf16[64,2048]{1,0:T(8,128)(2,1)} %collective-permute-done.15.refs_4_), channel_id=1, source_target_pairs={{0,4},{2,6},{4,0},{6,2},{8,12},{10,14},{12,8},{14,10},{16,20},{18,... | collective-permute-start | bytes 786440 | tf_op jit(solution)/shard_map/ppermute | solution.py:37
  155.3 6.0 %collective-permute-start.21 = (bf16[64,2048]{1,0:T(8,128)(2,1)S(1)}, bf16[64,2048]{1,0:T(8,128)(2,1)S(1)}, u32[]{:S(2)}, u32[]{:S(2)}) collective-permute-start(bf16[64,2048]{1,0:T(8,128)(2,1)S(1)} %copy-done.16), channel_id=1, source_target_pairs={{0,2},{2,0},{4,6},{6,4},{8,10},{10,8},{12,14},{14,12},{16,18},{18,... | collective-permute-start | bytes 786440 | tf_op jit(solution)/shard_map/ppermute | solution.py:37
  155.4 6.5 %collective-permute-start.23 = (bf16[64,2048]{1,0:T(8,128)(2,1)S(1)}, bf16[64,2048]{1,0:T(8,128)(2,1)S(1)}, u32[]{:S(2)}, u32[]{:S(2)}) collective-permute-start(bf16[64,2048]{1,0:T(8,128)(2,1)S(1)} %collective-permute-done.16.refs_2_), channel_id=1, source_target_pairs={{0,2},{2,0},{4,6},{6,4},{8,10},{10,8},{12,14},{14,12},{16,18},{18,... | collective-permute-start | bytes 786440 | tf_op jit(solution)/shard_map/ppermute | solution.py:37
  155.9 8.4 %collective-permute-start.24 = (bf16[128,2048]{1,0:T(8,128)(2,1)S(1)}, bf16[128,2048]{1,0:T(8,128)(2,1)S(1)}, u32[]{:S(2)}, u32[]{:S(2)}) collective-permute-start(bf16[128,2048]{1,0:T(8,128)(2,1)S(1)} %collective-permute-done.20.refs_3_), channel_id=1, source_target_pairs={{0,2},{2,0},{4,6},{6,4},{8,10},{10,8},{12,14},{14,12},{16,18},{18,... | collective-permute-start | bytes 1572872 | tf_op jit(solution)/shard_map/ppermute | solution.py:37
  161.3 3.0 collective-permute-start.27
  161.3 3.0 collective-permute-start.25
  161.8 2.5 collective-permute-start.22
  162.6 1.8 collective-permute-start.26
  220.2 10.0 %collective-permute-start.29 = (bf16[512,2048]{1,0:T(8,128)(2,1)}, bf16[512,2048]{1,0:T(8,128)(2,1)S(1)}, u32[]{:S(2)}, u32[]{:S(2)}) collective-permute-start(bf16[512,2048]{1,0:T(8,128)(2,1)} %get-tuple-element.68), channel_id=1, source_target_pairs={{0,2},{2,0},{4,6},{6,4},{8,10},{10,8},{12,14},{14,12},{16,18},{18,... | collective-permute-start | bytes 6291464 | tf_op jit(solution)/shard_map/ppermute | solution.py:37
  223.6 39.4 %collective-permute-start.33 = (bf16[16,32,1664]{2,1,0:T(8,128)(2,1)}, bf16[16,32,1664]{2,1,0:T(8,128)(2,1)}, u32[]{:S(2)}, u32[]{:S(2)}) collective-permute-start(bf16[16,32,1664]{2,1,0:T(8,128)(2,1)} %dynamic-slice_bitcast_fusion), channel_id=1, source_target_pairs={{0,1},{1,0},{2,3},{3,2},{4,5},{5,4},{6,7},{7,6},{8,9},{9,8},{10,11... | collective-permute-start | bytes 5111816 | tf_op jit(solution)/shard_map/ppermute | solution.py:855
  231.8 19.4 %collective-permute-start.30 = (bf16[192,2048]{1,0:T(8,128)(2,1)S(1)}, bf16[192,2048]{1,0:T(8,128)(2,1)}, u32[]{:S(2)}, u32[]{:S(2)}) collective-permute-start(bf16[192,2048]{1,0:T(8,128)(2,1)S(1)} %pad_maximum_fusion.1), channel_id=1, source_target_pairs={{0,4},{2,6},{4,0},{6,2},{8,12},{10,14},{12,8},{14,10},{16,20},{18,... | collective-permute-start | bytes 2359304 | tf_op jit(solution)/shard_map/ppermute | solution.py:37
  253.1 20.4 %collective-permute-start.32 = (bf16[64,2048]{1,0:T(8,128)(2,1)S(1)}, bf16[64,2048]{1,0:T(8,128)(2,1)S(1)}, u32[]{:S(2)}, u32[]{:S(2)}) collective-permute-start(bf16[64,2048]{1,0:T(8,128)(2,1)S(1)} %get-tuple-element.142), channel_id=1, source_target_pairs={{0,16},{2,18},{4,20},{6,22},{8,24},{10,26},{12,28},{14,30},{16,0},... | collective-permute-start | bytes 786440 | tf_op jit(solution)/shard_map/ppermute | solution.py:37
  258.6 14.9 %collective-permute-start.31 = (bf16[64,2048]{1,0:T(8,128)(2,1)S(1)}, bf16[64,2048]{1,0:T(8,128)(2,1)S(1)}, u32[]{:S(2)}, u32[]{:S(2)}) collective-permute-start(bf16[64,2048]{1,0:T(8,128)(2,1)S(1)} %get-tuple-element.147), channel_id=1, source_target_pairs={{0,4},{2,6},{4,0},{6,2},{8,12},{10,14},{12,8},{14,10},{16,20},{18,... | collective-permute-start | bytes 786440 | tf_op jit(solution)/shard_map/ppermute | solution.py:37
  260.0 13.5 %collective-permute-start.34 = (bf16[64,2048]{1,0:T(8,128)(2,1)S(1)}, bf16[64,2048]{1,0:T(8,128)(2,1)S(1)}, u32[]{:S(2)}, u32[]{:S(2)}) collective-permute-start(bf16[64,2048]{1,0:T(8,128)(2,1)S(1)} %get-tuple-element.141), channel_id=1, source_target_pairs={{0,24},{2,26},{4,28},{6,30},{8,0},{10,2},{12,4},{14,6},{16,8},{18,... | collective-permute-start | bytes 786440 | tf_op jit(solution)/shard_map/ppermute | solution.py:37
  261.7 15.5 %collective-permute-start.35 = (bf16[64,2048]{1,0:T(8,128)(2,1)S(1)}, bf16[64,2048]{1,0:T(8,128)(2,1)S(1)}, u32[]{:S(2)}, u32[]{:S(2)}) collective-permute-start(bf16[64,2048]{1,0:T(8,128)(2,1)S(1)} %get-tuple-element.140), channel_id=1, source_target_pairs={{0,8},{2,10},{4,12},{6,14},{8,16},{10,18},{12,20},{14,22},{16,24},... | collective-permute-start | bytes 786440 | tf_op jit(solution)/shard_map/ppermute | solution.py:37
  304.1 17.9 %collective-permute-start.36 = (bf16[1024,1024]{1,0:T(8,128)(2,1)}, bf16[1024,1024]{1,0:T(8,128)(2,1)}, u32[]{:S(2)}, u32[]{:S(2)}) collective-permute-start(bf16[1024,1024]{1,0:T(8,128)(2,1)} %get-tuple-element.80), channel_id=1, source_target_pairs={{0,2},{2,0},{4,6},{6,4},{8,10},{10,8},{12,14},{14,12},{16,18},{18,... | collective-permute-start | bytes 6291464 | tf_op jit(solution)/shard_map/ppermute | solution.py:37
  307.4 64.7 %all-to-all-start.2 = ((bf16[16,32,1664]{2,1,0:T(8,128)(2,1)}), bf16[16,32,1664]{2,1,0:T(8,128)(2,1)S(1)}, u32[]{:S(2)}, u32[]{:S(2)}) async-start(bf16[16,32,1664]{2,1,0:T(8,128)(2,1)} %fusion), calls=%async_computation.3 | async-start | bytes 3407872 | tf_op jit(solution)/shard_map/all_to_all | solution.py:865
  324.1 32.3 %collective-permute-start.38 = (bf16[384,1024]{1,0:T(8,128)(2,1)S(1)}, bf16[384,1024]{1,0:T(8,128)(2,1)S(1)}, u32[]{:S(2)}, u32[]{:S(2)}) collective-permute-start(bf16[384,1024]{1,0:T(8,128)(2,1)S(1)} %pad_maximum_fusion.2), channel_id=1, source_target_pairs={{0,4},{2,6},{4,0},{6,2},{8,12},{10,14},{12,8},{14,10},{16,20},{18,... | collective-permute-start | bytes 2359304 | tf_op jit(solution)/shard_map/ppermute | solution.py:37
  326.0 32.2 %collective-permute-start.43 = (bf16[16,32,256]{2,1,0:T(8,128)(2,1)S(1)}, bf16[16,32,256]{2,1,0:T(8,128)(2,1)S(1)}, u32[]{:S(2)}, u32[]{:S(2)}) collective-permute-start(bf16[16,32,256]{2,1,0:T(8,128)(2,1)S(1)} %dynamic-slice_bitcast_fusion.1), channel_id=1, source_target_pairs={{0,1},{1,0},{2,3},{3,2},{4,5},{5,4},{6,7},{7,6},{8,9},{9,8},{10,11... | collective-permute-start | bytes 786440 | tf_op jit(solution)/shard_map/ppermute | solution.py:855
  358.3 1.4 collective-permute-start.44
  359.8 6.4 %collective-permute-start.45 = (bf16[4,2,32,256]{3,2,1,0:T(8,128)(2,1)S(1)}, bf16[4,2,32,256]{3,2,1,0:T(8,128)(2,1)S(1)}, u32[]{:S(2)}, u32[]{:S(2)}) collective-permute-start(bf16[4,2,32,256]{3,2,1,0:T(8,128)(2,1)S(1)} %bitcast.110), channel_id=1, source_target_pairs={{0,4},{2,6},{4,0},{6,2},{8,12},{10,14},{12,8},{14,10},{16,20},{18,... | collective-permute-start | bytes 393224 | tf_op jit(solution)/shard_map/ppermute | solution.py:37
  361.7 34.5 %collective-permute-start.37 = (bf16[128,1024]{1,0:T(8,128)(2,1)S(1)}, bf16[128,1024]{1,0:T(8,128)(2,1)S(1)}, u32[]{:S(2)}, u32[]{:S(2)}) collective-permute-start(bf16[128,1024]{1,0:T(8,128)(2,1)S(1)} %get-tuple-element.143), channel_id=1, source_target_pairs={{0,4},{2,6},{4,0},{6,2},{8,12},{10,14},{12,8},{14,10},{16,20},{18,... | collective-permute-start | bytes 786440 | tf_op jit(solution)/shard_map/ppermute | solution.py:37
  362.4 33.8 %collective-permute-start.39 = (bf16[128,1024]{1,0:T(8,128)(2,1)S(1)}, bf16[128,1024]{1,0:T(8,128)(2,1)}, u32[]{:S(2)}, u32[]{:S(2)}) collective-permute-start(bf16[128,1024]{1,0:T(8,128)(2,1)S(1)} %get-tuple-element.137), channel_id=1, source_target_pairs={{0,16},{2,18},{4,20},{6,22},{8,24},{10,26},{12,28},{14,30},{16,0},... | collective-permute-start | bytes 786440 | tf_op jit(solution)/shard_map/ppermute | solution.py:37
  366.9 26.0 %copy-start.14 = (f32[128,1024]{1,0:T(8,128)S(1)}, f32[128,1024]{1,0:T(8,128)}, u32[]{:S(2)}) copy-start(f32[128,1024]{1,0:T(8,128)} %get-tuple-element.65) | copy-start | bytes 1572868
  366.9 13.2 %collective-permute-start.46 = (bf16[4,32,256]{2,1,0:T(8,128)(2,1)}, bf16[4,32,256]{2,1,0:T(8,128)(2,1)}, u32[]{:S(2)}, u32[]{:S(2)}) collective-permute-start(bf16[4,32,256]{2,1,0:T(8,128)(2,1)} %get-tuple-element.157), channel_id=1, source_target_pairs={{0,24},{2,26},{4,28},{6,30},{8,0},{10,2},{12,4},{14,6},{16,8},{18,... | collective-permute-start | bytes 196616 | tf_op jit(solution)/shard_map/ppermute | solution.py:37
  368.9 16.5 %collective-permute-start.47 = (bf16[4,32,256]{2,1,0:T(8,128)(2,1)}, bf16[4,32,256]{2,1,0:T(8,128)(2,1)}, u32[]{:S(2)}, u32[]{:S(2)}) collective-permute-start(bf16[4,32,256]{2,1,0:T(8,128)(2,1)} %get-tuple-element.158), channel_id=1, source_target_pairs={{0,16},{2,18},{4,20},{6,22},{8,24},{10,26},{12,28},{14,30},{16,0},... | collective-permute-start | bytes 196616 | tf_op jit(solution)/shard_map/ppermute | solution.py:37
  372.0 13.4 %collective-permute-start.48 = (bf16[4,32,256]{2,1,0:T(8,128)(2,1)}, bf16[4,32,256]{2,1,0:T(8,128)(2,1)}, u32[]{:S(2)}, u32[]{:S(2)}) collective-permute-start(bf16[4,32,256]{2,1,0:T(8,128)(2,1)} %get-tuple-element.155), channel_id=1, source_target_pairs={{0,8},{2,10},{4,12},{6,14},{8,16},{10,18},{12,20},{14,22},{16,24},... | collective-permute-start | bytes 196616 | tf_op jit(solution)/shard_map/ppermute | solution.py:37
  377.2 20.2 %copy-start.4 = (bf16[1,128,1024]{2,1,0:T(8,128)(2,1)S(1)}, bf16[1,128,1024]{2,1,0:T(8,128)(2,1)}, u32[]{:S(2)}) copy-start(bf16[1,128,1024]{2,1,0:T(8,128)(2,1)} %param.17) | copy-start | bytes 786436
  380.1 16.2 %collective-permute-start.41 = (bf16[128,1024]{1,0:T(8,128)(2,1)S(1)}, bf16[128,1024]{1,0:T(8,128)(2,1)S(1)}, u32[]{:S(2)}, u32[]{:S(2)}) collective-permute-start(bf16[128,1024]{1,0:T(8,128)(2,1)S(1)} %get-tuple-element.139), channel_id=1, source_target_pairs={{0,24},{2,26},{4,28},{6,30},{8,0},{10,2},{12,4},{14,6},{16,8},{18,... | collective-permute-start | bytes 786440 | tf_op jit(solution)/shard_map/ppermute | solution.py:37
  385.4 12.1 %collective-permute-start.42 = (bf16[128,1024]{1,0:T(8,128)(2,1)S(1)}, bf16[128,1024]{1,0:T(8,128)(2,1)S(1)}, u32[]{:S(2)}, u32[]{:S(2)}) collective-permute-start(bf16[128,1024]{1,0:T(8,128)(2,1)S(1)} %get-tuple-element.138), channel_id=1, source_target_pairs={{0,8},{2,10},{4,12},{6,14},{8,16},{10,18},{12,20},{14,22},{16,24},... | collective-permute-start | bytes 786440 | tf_op jit(solution)/shard_map/ppermute | solution.py:37
  390.2 5.4 %collective-permute-start.40 = (f32[32,1024]{1,0:T(8,128)S(1)}, f32[32,1024]{1,0:T(8,128)S(1)}, u32[]{:S(2)}, u32[]{:S(2)}) collective-permute-start(f32[32,1024]{1,0:T(8,128)S(1)} %dynamic-slice_bitcast_fusion.2), channel_id=1, source_target_pairs={{0,1},{1,0},{2,3},{3,2},{4,5},{5,4},{6,7},{7,6},{8,9},{9,8},{10,11... | collective-permute-start | bytes 393224 | tf_op jit(solution)/shard_map/ppermute | solution.py:855
  (22 other events, 54.3 us)
Sparse Core Ops, SparseCore 0:
  11.1 73.7 all-gather.3
  87.2 78.4 all-gather.5
  253.3 109.3 reduce-scatter.1
